TPU v7x, 32 devices: a whole 2x2x4 slice. The times are simulated.
32 devices in a mesh: dp: 16 (over z, x, core), ctx: 2 (over y).
Axes of the slice: x: 2, y: 2, z: 4, core: 2. Of those that a mesh axis runs over, the one named last changes fastest.
Arguments:
- tokens: bfloat16 [16, 256, 960], P('dp', 'ctx'), may hold values from -6 to 6
- segment_ids: int32 [16, 256], P('dp', 'ctx'), may hold values from 0 to 3, never falling along the last dimension, each value on 1 to 128 neighbouring positions
- norm_gains: float32 [2, 960], P(None, 'dp'), may hold values from 0.5 to 1.5
- w_query: bfloat16 [960, 960], P('dp', 'ctx'), may hold values from -0.1875 to 0.1875
- w_key: bfloat16 [960, 320], P('dp', 'ctx'), may hold values from -0.1875 to 0.1875
- w_value: bfloat16 [960, 320], P('dp', 'ctx'), may hold values from -0.1875 to 0.1875
- w_out: bfloat16 [960, 960], P('dp', 'ctx'), may hold values from -0.75 to 0.75
- w_gate: bfloat16 [960, 2560], P('dp', 'ctx'), may hold values from -0.1875 to 0.1875
- w_up: bfloat16 [960, 2560], P('dp', 'ctx'), may hold values from -0.1875 to 0.1875
- w_down: bfloat16 [2560, 960], P('dp', 'ctx'), may hold values from -0.125 to 0.125
- cotangent: bfloat16 [16, 256, 960], P('dp', 'ctx'), may hold values from -6 to 6
Outputs:
- block_output: bfloat16 [16, 256, 960], P('dp', 'ctx')
- input_grad: float32 [16, 256, 960], P('dp', 'ctx')
- query_grad: float32 [960, 960], P('dp', 'ctx')
- key_grad: float32 [960, 320], P('dp', 'ctx')
- value_grad: float32 [960, 320], P('dp', 'ctx')
- out_grad: float32 [960, 960], P('dp', 'ctx')
- gate_grad: float32 [960, 2560], P('dp', 'ctx')
- up_grad: float32 [960, 2560], P('dp', 'ctx')
- down_grad: float32 [2560, 960], P('dp', 'ctx')
- gain_grad: float32 [2, 960], P(None, 'dp')
Inputs may be any that keep to these rules, and one draw needn't show every extreme that they name: `segment_ids`: along each sequence the segment number never falls; each segment holds 1 to 128 tokens, and one segment of each sequence holds exactly that many.
All inputs are finite; a program needn't handle non-finite values.
Results may differ from a plain program's by a relative error of at most 0.034.
Values may be sent and summed in bfloat16 or wider, within the bound.
No kernel may reach another device: no remote copies, remote signals or barrier semaphores. Data moves between devices by JAX's collectives and lax.ppermute only.
A program may use at most 192 MiB of HBM per device.

v0:
```python
import functools
import math

import jax
import jax.numpy as jnp
from jax import lax
from jax.experimental import pallas as pl
from jax.experimental.pallas import tpu as pltpu
from jax.sharding import PartitionSpec as P


H = 15
KV = 5
HD = 64


norm_eps = 1e-05
rope_base = 100000.0

AXES = ("dp", "ctx")


def normed(hidden, scales):
    factor = lax.rsqrt(jnp.mean(hidden * hidden, axis=-1, keepdims=True) + norm_eps)
    return hidden * factor * scales


def rope_tables(amount, offset, head_size):
    middle = head_size // 2
    inverse_rates = rope_base ** (-(jnp.arange(middle, dtype=jnp.float32) * 2.0) / head_size)
    places = (offset + jnp.arange(amount, dtype=jnp.int32)).astype(jnp.float32)
    angles = places[:, None] * inverse_rates[None, :]
    return (jnp.cos(angles)[:, None, :], jnp.sin(angles)[:, None, :])


def rotate(values, cosine, sine):
    middle = values.shape[-1] // 2
    first_half = values[..., :middle]
    second_half = values[..., middle:]
    return jnp.concatenate(
        [first_half * cosine - second_half * sine, second_half * cosine + first_half * sine],
        axis=-1,
    )


def unrotate(values, cosine, sine):
    middle = values.shape[-1] // 2
    first_half = values[..., :middle]
    second_half = values[..., middle:]
    return jnp.concatenate(
        [first_half * cosine + second_half * sine, second_half * cosine - first_half * sine],
        axis=-1,
    )


def matmul(left, right):
    return jnp.dot(left, right, preferred_element_type=jnp.float32)


def score_block(grouped, key_grid, scale_factor):
    return (
        jnp.einsum("tkgd,skd->kgts", grouped, key_grid, preferred_element_type=jnp.float32)
        * scale_factor
    )


def probabilities(scores, allowed, log_total):
    return jnp.where(allowed, jnp.exp(scores - log_total), 0.0)


bf16 = jnp.bfloat16
f32 = jnp.float32


class Links:
    def __init__(self):
        self.dp = lax.axis_size("dp")
        self.nz = self.dp // 4
        index = lax.axis_index("dp")
        self.y = lax.axis_index("ctx")
        self.c = index % 2
        self.x = (index // 2) % 2
        self.z = index // 4

    def _permute(self, value, target):
        pairs = []
        for z in range(self.nz):
            for x in range(2):
                for c in range(2):
                    for y in range(2):
                        z2, x2, c2, y2 = target(z, x, c, y)
                        pairs.append(
                            (((z * 2 + x) * 2 + c) * 2 + y, ((z2 * 2 + x2) * 2 + c2) * 2 + y2)
                        )
        return lax.ppermute(value, AXES, pairs)

    def core(self, value):
        return self._permute(value, lambda z, x, c, y: (z, x, 1 - c, y))

    def over_x(self, value):
        return self._permute(value, lambda z, x, c, y: (z, 1 - x, c, y))

    def over_y(self, value):
        return self._permute(value, lambda z, x, c, y: (z, x, c, 1 - y))

    def over_z(self, value, step):
        return self._permute(value, lambda z, x, c, y: ((z + step) % self.nz, x, c, y))

    def order(self, flag, own, other, axis):
        return jnp.where(
            flag == 0,
            jnp.concatenate([own, other], axis=axis),
            jnp.concatenate([other, own], axis=axis),
        )

    def gather_z(self, block):
        parts = [block] + [self.over_z(block, k) for k in range(1, self.nz)]
        slots = []
        for slot in range(self.nz):
            distance = (self.z - slot) % self.nz
            value = parts[0]
            for k in range(1, self.nz):
                value = jnp.where(distance == k, parts[k], value)
            slots.append(value)
        return jnp.stack(slots, axis=1)

    def spread(self, line):
        by_x = self.over_x(line)
        by_y = self.over_y(line)
        corners = self.over_y(by_x[0]), self.over_x(by_y[1])
        return line, by_x, by_y, *corners

    def reduce(self, parts):
        send_y, send_x, by_x, by_y, own = parts
        got_y = self.over_y(send_y)
        got_x = self.over_x(send_x)
        onward_x = (by_x.astype(f32) + got_y[1].astype(f32)).astype(bf16)
        onward_y = (by_y.astype(f32) + got_x[1].astype(f32)).astype(bf16)
        last_x = self.over_x(onward_x)
        last_y = self.over_y(onward_y)
        line = jnp.stack(
            [
                own[0].astype(f32) + got_y[0].astype(f32) + last_x.astype(f32),
                own[1].astype(f32) + got_x[0].astype(f32) + last_y.astype(f32),
            ],
            axis=1,
        )
        low = line.astype(bf16)
        total = lax.dynamic_index_in_dim(line, self.z, 0, keepdims=False)
        for k in range(1, self.nz):
            block = lax.dynamic_index_in_dim(low, (self.z + k) % self.nz, 0, keepdims=False)
            arrived = self.over_z(block, k)
            total = total + arrived.astype(f32)
        return total


def pick(flag, pair):
    return jnp.where(flag == 0, pair[0], pair[1])


def padded_columns(count, block, wide, offset, total):
    target = jnp.arange(count // block * wide, dtype=jnp.int32)[None, :]
    lane = target % wide
    source = jnp.where(lane < block, offset + target // wide * block + lane, -1)
    source = lax.optimization_barrier(source)
    return (jnp.arange(total, dtype=jnp.int32)[:, None] == source).astype(bf16)


def dot_t(left, right):
    return lax.dot_general(left, right, (((0,), (0,)), ((), ())), preferred_element_type=f32)


def dot_nt(left, right):
    return lax.dot_general(left, right, (((1,), (1,)), ((), ())), preferred_element_type=f32)


def swapped(value):
    lanes = value.shape[1]
    lane = lax.broadcasted_iota(jnp.int32, value.shape, 1) % HD
    up = pltpu.roll(value, lanes - HD // 2, 1)
    down = pltpu.roll(value, HD // 2, 1)
    return jnp.where(lane < HD // 2, up, down)


def wide_table(table, lanes):
    return jnp.concatenate([table] * (lanes // table.shape[1]), axis=1)


def attention_forward(
    dims, place_ref, pad_ref, pick_ref, mine_ref, facing_ref, allowed_ref, cos_ref, sin_ref, *refs
):
    nz, rows, width, q_cols, k_cols = dims
    pieces, refs = refs[:10], refs[10:]
    (w_ref, wo_ref, gains_ref, x_ref, q_ref, k_ref, v_ref, p_ref, att_ref, middle_ref, second_ref) = refs[:11]
    wide_q, wide_k = refs[11:]
    c, x, y = place_ref[0], place_ref[1], place_ref[2]
    tokens = mine_ref.shape[0]
    for own in range(2):
        line, by_x, by_y, corner_0, corner_1 = pieces[own * 5 : own * 5 + 5]
        which = jnp.where(c == own, 0, 1)

        def store(t, y, z, x, piece, which=which):
            w_ref[which, y, z, x, t * 64 : (t + 1) * 64, :] = piece

        assemble(store, x, y, nz, line, by_x, by_y, corner_0, corner_1)
    gains = [[], []]
    for z in range(nz):
        for p in range(2):
            low, high = (w_ref[0, 0, z, p, at - 8 : at, :][4:5].astype(f32) for at in (64, 128))
            for i in range(2):
                gains[i].append((low + high)[:, i * 128 : (i + 1) * 128])
    gains = [jnp.concatenate(g, axis=1) for g in gains]
    gains_ref[...] = jnp.concatenate(gains + [jnp.zeros_like(gains[0])] * 6, axis=0)
    blank = jnp.zeros((64 - rows, w_ref.shape[-1]), bf16)

    @pl.loop(0, nz)
    def _(z):
        for s in range(2):
            for half in range(2):
                for p in range(2):
                    for at in (rows, rows + 64):
                        w_ref[s, half, z, p, at : at + 64 - rows, :] = blank

    hidden = matmul(jnp.concatenate([mine_ref[...], facing_ref[...]], axis=0), pad_ref[...])
    factor = lax.rsqrt(jnp.sum(hidden * hidden, axis=1, keepdims=True) / width + norm_eps)
    first = (hidden * factor * gains[0]).astype(bf16)
    x_ref[...] = first
    deep = nz * 2 * 128
    wide_q[...] = jnp.zeros_like(wide_q)
    wide_k[...] = jnp.zeros_like(wide_k)
    for half in range(2):
        both = matmul(first, w_ref[0, half].reshape(deep, q_cols + k_cols))
        wide_q[:, half * q_cols : (half + 1) * q_cols] = both[:tokens, :q_cols]
        wide_k[:, half * k_cols : (half + 1) * k_cols] = both[:, q_cols:]
        values = matmul(first, w_ref[1, half].reshape(deep, q_cols + k_cols)[:, :k_cols])
        v_ref[:, half * k_cols : (half + 1) * k_cols] = values.astype(bf16)
    cosine, sine = cos_ref[...], sin_ref[...]
    lanes = wide_q.shape[1]
    query = wide_q[...]
    query = query * wide_table(cosine[:tokens], lanes) + swapped(query) * wide_table(
        sine[:tokens], lanes
    )
    q_ref[...] = query.astype(bf16)
    lanes = wide_k.shape[1]
    keys = wide_k[...]
    keys = keys * wide_table(cosine, lanes) + swapped(keys) * wide_table(sine, lanes)
    k_ref[...] = keys.astype(bf16)
    groups = H // KV
    allowed = jnp.concatenate([allowed_ref[...]] * groups, axis=0) > 0
    for g in range(KV):
        heads = [
            q_ref[:, (g * groups + i) * HD : (g * groups + i + 1) * HD] for i in range(groups)
        ]
        scores = dot_nt(jnp.concatenate(heads, axis=0), k_ref[:, g * HD : (g + 1) * HD])
        scores = scores * (1.0 / math.sqrt(HD))
        totals = jnp.sum(jnp.where(allowed, jnp.exp(scores), 0.0), axis=1, keepdims=True)
        probs = jnp.where(allowed, jnp.exp(scores - jnp.log(totals)), 0.0)
        p_ref[g] = probs
        out = matmul(probs.astype(bf16), v_ref[:, g * HD : (g + 1) * HD])
        for i in range(groups):
            j = g * groups + i
            wide_q[:, j * HD : (j + 1) * HD] = out[i * tokens : (i + 1) * tokens]
    attended = matmul(wide_q[:, :width].astype(bf16), pad_ref[...]).astype(bf16)
    att_ref[...] = attended
    outs = []
    for half in range(2):
        w_out = matmul(w_ref[1, half].reshape(deep, q_cols + k_cols), pick_ref[...]).astype(bf16)
        wo_ref[half] = w_out
        outs.append(matmul(attended, w_out))
    middle = hidden[:tokens] + jnp.concatenate(outs, axis=1)
    middle_ref[...] = middle
    factor = lax.rsqrt(jnp.sum(middle * middle, axis=1, keepdims=True) / width + norm_eps)
    second_ref[...] = (middle * factor * gains[1]).astype(bf16)


def deal(item, x, y, nz, send_y, send_x, by_x, by_y, own):
    @pl.loop(0, nz)
    def _(z):
        for d in range(2):
            send_y[d, z] = item(0, 1 - y, z, x ^ d)
            send_x[d, z] = item(1, y ^ d, z, 1 - x)
            own[d, z] = item(d, y, z, x)
        by_x[z] = item(0, y, z, 1 - x)
        by_y[z] = item(1, 1 - y, z, x)


def pack_shapes(nz, *block):
    two, one = ((2, nz, *block), bf16), ((nz, *block), bf16)
    return [two, two, one, one, two]


def assemble(store, x, y, nz, line, by_x, by_y, corner_0, corner_1):
    @pl.loop(0, nz)
    def _(z):
        for t in range(2):
            corner = (corner_0, corner_1)[t]
            for dy in range(2):
                for dx in range(2):
                    piece = corner[z] if dy and dx else (line, by_x, by_y)[dx + 2 * dy][t, z]
                    store(t, y ^ dy, z, x ^ dx, piece)


def assemble_gate_up(w_ref, x, y, nz, gate_parts, up_parts):
    for which, parts in enumerate((gate_parts, up_parts)):

        def store(t, y, z, x, piece, which=which):
            w_ref[which, y, z, x, t * 64 : (t + 1) * 64, :] = piece

        assemble(store, x, y, nz, *parts)


def feed_forward(dims, place_ref, second_ref, got_ref, cot_ref, *refs):
    nz, ff_rows = dims
    x, y = place_ref[1], place_ref[2]
    (gate_ref, up_ref, mixed_ref, *dealt), (w_ref, sums) = refs[10:18], refs[18:]
    assemble_gate_up(w_ref, x, y, nz, refs[:5], refs[5:10])
    pair = jnp.concatenate([second_ref[...], got_ref[...]], axis=0)
    deep, n = nz * 2 * 128, w_ref.shape[-1]
    part, count = ff_rows // 2, n // ff_rows

    @pl.loop(0, 2)
    def _(half):
        gate = matmul(pair, w_ref[0, half].reshape(deep, n))
        upward = matmul(pair, w_ref[1, half].reshape(deep, n))
        gate_ref[half] = gate
        up_ref[half] = upward
        sigma = 1.0 / (1.0 + jnp.exp(-gate))
        mixed = (gate * sigma * upward).astype(bf16)
        mixed_ref[half] = mixed
        for columns in range(2):
            grads = dot_t(mixed, cot_ref[columns]).astype(bf16)
            for block in range(count):
                for t in range(2):
                    at = block * ff_rows + t * part
                    z = half * (count // 2) + block // 2
                    sums[t, columns, z, block % 2] = grads[at : at + part]

    deal(lambda t, y, z, x: sums[t, y, z, x], x, y, nz, *dealt)


def feed_backward(dims, place_ref, pad_ref, second_ref, got_ref, cot_ref, gate_ref, up_ref, mixed_ref, *refs):
    nz, ff_rows = dims
    x, y = place_ref[1], place_ref[2]
    (out_ref, out_away_ref, back_ref, back_away_ref, *dealt) = refs[15:24]
    (w_ref, d_ref, sums, back, out) = refs[24:]
    part = ff_rows // 2

    def store(t, y, z, x, piece):
        d_ref[y, z, x, t * part : (t + 1) * part, :] = piece

    assemble(store, x, y, nz, *refs[10:15])
    assemble_gate_up(w_ref, x, y, nz, refs[:5], refs[5:10])
    tokens = second_ref.shape[0]
    pair = jnp.concatenate([second_ref[...], got_ref[...]], axis=0)
    deep, n = nz * 2 * 128, w_ref.shape[-1]
    lanes = out.shape[1] // 2
    back[...] = jnp.zeros_like(back)
    out[...] = jnp.zeros_like(out)

    @pl.loop(0, 2)
    def _(half):
        mine = pl.ds(half * (nz // 2), nz // 2)
        down = [d_ref[columns, mine].reshape(n, d_ref.shape[-1]) for columns in range(2)]
        gm = dot_nt(cot_ref[0], down[0]) + dot_nt(cot_ref[1], down[1])
        gate, upward = gate_ref[half], up_ref[half]
        sigma = 1.0 / (1.0 + jnp.exp(-gate))
        grad_gate = (gm * upward * sigma * (1.0 + gate * (1.0 - sigma))).astype(bf16)
        grad_up = (gm * (gate * sigma)).astype(bf16)
        for which, grad in enumerate((grad_gate, grad_up)):
            total = dot_t(pair, grad).astype(bf16)
            for z in range(nz):
                for p in range(2):
                    for t in range(2):
                        at = ((z * 2 + p) * 2 + t) * 64
                        sums[t, half, z, p, which] = total[at : at + 64]
            back[...] += dot_nt(grad, w_ref[which, half].reshape(deep, n))
        for columns in range(2):
            wide = matmul(down[columns], pad_ref[...]).astype(bf16)
            out[:, columns * lanes : (columns + 1) * lanes] += matmul(mixed_ref[half], wide)

    deal(lambda t, y, z, x: sums[t, y, z, x], x, y, nz, *dealt)
    back_ref[...] = back[:tokens]
    back_away_ref[...] = back[tokens:].astype(bf16)
    out_ref[...] = out[:tokens]
    out_away_ref[...] = out[tokens:].astype(bf16)


def attention_backward(
    dims, place_ref, pad_ref, cot_ref, mine_ref, facing_ref, cos_ref, sin_ref, back_ref, back_got_ref, w_ref, wo_ref,
    gains_ref, x_ref, q_ref, k_ref, v_ref, p_ref, att_ref, middle_ref, keep_ref, away_ref, grad_middle_ref, first_ref,
    first_away_ref, wide_q, wide_k, wide_v, wide_g, sums, lefts, rights, outs, back,
):
    nz, rows, width, q_cols, k_cols = dims
    c, x, y = place_ref[0], place_ref[1], place_ref[2]
    tokens = middle_ref.shape[0]
    deep = nz * 2 * 128
    pad = pad_ref[...]
    gains = gains_ref[...]
    middle = middle_ref[...]
    factor = lax.rsqrt(jnp.sum(middle * middle, axis=1, keepdims=True) / width + norm_eps)
    incoming = back_ref[...] + back_got_ref[...].astype(f32)
    gain_second = jnp.sum(incoming * middle * factor, axis=0, keepdims=True)
    scaled = incoming * gains[1:2]
    mean = jnp.sum(scaled * middle, axis=1, keepdims=True) / width
    grad_middle = (
        matmul(cot_ref[...], pad) + factor * scaled - middle * (factor * factor * factor * mean)
    )
    grad_middle_ref[...] = grad_middle
    branch = grad_middle.astype(bf16)
    half_lanes = wo_ref.shape[-1]
    grad_att = dot_nt(branch[:, :half_lanes], wo_ref[0]) + dot_nt(branch[:, half_lanes:], wo_ref[1])
    grad_att = dot_nt(grad_att.astype(bf16), pad).astype(bf16)
    groups = H // KV
    wide_q[...] = jnp.zeros_like(wide_q)
    wide_k[...] = jnp.zeros_like(wide_k)
    wide_g[:, :width] = grad_att
    for g in range(KV):
        at = slice(g * HD, (g + 1) * HD)
        heads = [slice((g * groups + i) * HD, (g * groups + i + 1) * HD) for i in range(groups)]
        grad = jnp.concatenate([wide_g[:, h] for h in heads], axis=0)
        query = jnp.concatenate([q_ref[:, h] for h in heads], axis=0)
        probs = p_ref[g]
        wide_v[:, at] = dot_t(probs.astype(bf16), grad)
        grad_probs = dot_nt(grad, v_ref[:, at])
        row = jnp.sum(probs * grad_probs, axis=1, keepdims=True)
        grad_scores = (probs * (grad_probs - row) * (1.0 / math.sqrt(HD))).astype(bf16)
        wide_k[:, at] = dot_t(grad_scores, query)
        out = matmul(grad_scores, k_ref[:, at])
        for i in range(groups):
            wide_q[:, heads[i]] = out[i * tokens : (i + 1) * tokens]
    cosine, sine = cos_ref[...], sin_ref[...]
    lanes = wide_q.shape[1]
    value = wide_q[...]
    value = value * wide_table(cosine[:tokens], lanes) - swapped(value) * wide_table(
        sine[:tokens], lanes
    )
    wide_q[...] = value
    lanes = wide_k.shape[1]
    value = wide_k[...]
    value = value * wide_table(cosine, lanes) - swapped(value) * wide_table(sine, lanes)
    wide_k[...] = value
    plain = dot_nt(branch, pad)
    first = x_ref[...]
    attended = att_ref[...]
    zeros_q = jnp.zeros((tokens, q_cols), f32)
    zeros_o = jnp.zeros((2 * tokens, q_cols), f32)
    zeros_v = jnp.zeros((tokens, k_cols), f32)
    n = q_cols + k_cols
    for half in range(2):
        of_q = jnp.concatenate([wide_q[:, half * q_cols : (half + 1) * q_cols], zeros_q], axis=0)
        of_k = wide_k[:, half * k_cols : (half + 1) * k_cols]
        of_v = wide_v[:, half * k_cols : (half + 1) * k_cols]
        of_o = plain[:, half * q_cols : (half + 1) * q_cols]
        lefts[half] = jnp.concatenate([of_q, of_k], axis=1).astype(bf16)
        rights[half] = jnp.concatenate([of_v, zeros_o], axis=1).astype(bf16)
        outs[half] = jnp.concatenate([zeros_v, of_o], axis=1).astype(bf16)
    back[...] = jnp.zeros_like(back)

    @pl.loop(0, 2)
    def _(half):
        left, right = lefts[half], rights[half]
        totals = (dot_t(first, left), dot_t(first, right) + dot_t(attended, outs[half]))
        for s in range(2):
            total = totals[s].astype(bf16)
            for z in range(nz):
                for p in range(2):
                    for t in range(2):
                        at = ((z * 2 + p) * 2 + t) * 64
                        sums[s, t, half, z, p] = total[at : at + 64]
            back[...] += dot_nt((left, right)[s], w_ref[s, half].reshape(deep, n))

    hidden = matmul(jnp.concatenate([mine_ref[...], facing_ref[...]], axis=0), pad)
    factor = lax.rsqrt(jnp.sum(hidden * hidden, axis=1, keepdims=True) / width + norm_eps)
    gain_first = jnp.sum(back[...] * hidden * factor, axis=0, keepdims=True)
    first_ref[...] = back[:tokens]
    first_away_ref[...] = back[tokens:].astype(bf16)
    for z in range(nz):
        for p in range(2):
            lane = slice((z * 2 + p) * 128, (z * 2 + p + 1) * 128)
            gain_row = jnp.concatenate(
                [gain_first[:, lane], gain_second[:, lane], jnp.zeros((1, n - 256), f32)], axis=1
            )
            gain_rows = jnp.concatenate(
                [gain_row, jnp.zeros((63 - rows, n), f32)], axis=0
            ).astype(bf16)
            for half in range(2):
                for s in range(2):
                    for t in range(2):
                        sums[s, t, half, z, p, rows:64, :] = gain_rows
    for which, ref in ((c, keep_ref), (1 - c, away_ref)):
        views = (ref.at[0:2], ref.at[2:4], ref.at[4], ref.at[5], ref.at[6:8])
        deal(lambda t, y, z, x, s=which: sums[s, t, y, z, x], x, y, nz, *views)


def run_kernel(body, inputs, outs, scratch):
    moved = sum(math.prod(a.shape) * a.dtype.itemsize for a in inputs)
    vmem = pl.BlockSpec(memory_space=pltpu.VMEM)
    return pl.pallas_call(
        body,
        out_shape=[jax.ShapeDtypeStruct(shape, kind) for shape, kind in outs],
        in_specs=[pl.BlockSpec(memory_space=pltpu.SMEM)] + [vmem] * (len(inputs) - 1),
        out_specs=[vmem] * len(outs),
        scratch_shapes=scratch,
        compiler_params=pltpu.CompilerParams(vmem_limit_bytes=60 << 20),
        cost_estimate=pl.CostEstimate(flops=2 * 10**9, bytes_accessed=moved, transcendentals=0),
    )(*inputs)


def fast_pass(
    tokens, segment_ids, norm_gains, w_query, w_key, w_value, w_out, w_gate, w_up, w_down, cotangent
):
    net = Links()
    nz, c, x, y = net.nz, net.c, net.x, net.y
    local_rows = tokens.shape[1]
    width = tokens.shape[2]
    rows = w_query.shape[0]
    groups = H // KV
    q_cols, k_cols, o_cols = w_query.shape[1], w_key.shape[1], w_out.shape[1]
    attn_cols = q_cols + k_cols
    ff_rows = w_down.shape[0]
    half_ff = w_gate.shape[1] // 2

    mine = tokens[0]
    segments_mine = segment_ids[0]
    segment_row = jnp.pad(
        segments_mine[None].astype(bf16), ((0, 7), (0, width - local_rows))
    )
    facing_pack = net.over_y(jnp.concatenate([mine, segment_row], axis=0))
    facing = facing_pack[:local_rows]
    segments_facing = facing_pack[local_rows, :local_rows].astype(jnp.int32)
    incoming = cotangent[0]
    incoming_got = net.core(incoming)
    incoming_pair = jnp.concatenate([incoming, incoming_got], axis=0)

    def by_core(w):
        starts = range(0, 2 * half_ff, 2 * ff_rows)
        return [
            jnp.concatenate(
                [w[:, at + i * ff_rows : at + (i + 1) * ff_rows] for at in starts], axis=1
            )
            for i in range(2)
        ]

    qk = jnp.concatenate([w_query, w_key], axis=1)
    vo = jnp.concatenate([w_value, w_out], axis=1)
    gate_half, up_half = by_core(w_gate), by_core(w_up)
    gains_row = jnp.pad(norm_gains.astype(bf16), ((0, 0), (0, 64 - rows)))
    gains_row = net.order(c, gains_row, jnp.zeros_like(gains_row), 1).reshape(1, 256)
    gains_row = jnp.pad(gains_row, ((0, 63 - rows), (0, attn_cols - 256)))

    def with_gains(w):
        return jnp.concatenate([w, gains_row], axis=0)

    def tall(w):
        return jnp.pad(w, ((0, 64 - rows), (0, 0)))

    got = net.core(
        jnp.stack(
            [
                with_gains(pick(c, (vo, qk))),
                tall(pick(c, (gate_half[1], gate_half[0]))),
                tall(pick(c, (up_half[1], up_half[0]))),
            ]
        )
    )
    attn_rows = 64

    def chip_pack(own, other):
        return net.order(c, own[None], other[None], 0)

    attn_pack = chip_pack(with_gains(pick(c, (qk, vo))), got[0])
    gate_pack = chip_pack(tall(pick(c, gate_half)), got[1])
    up_pack = chip_pack(tall(pick(c, up_half)), got[2])
    down_pack = w_down.reshape(2, ff_rows // 2, w_down.shape[1])

    attn_line = net.gather_z(attn_pack)
    gate_line = net.gather_z(gate_pack)
    up_line = net.gather_z(up_pack)
    down_line = net.gather_z(down_pack)
    attn_own = net.spread(attn_line)
    attn_other = [net.core(piece) for piece in attn_own]
    gate_parts = net.spread(gate_line)
    up_parts = net.spread(up_line)
    down_parts = net.spread(down_line)

    place = jnp.stack([c, x, y]).astype(jnp.int32)
    both_rows = 2 * local_rows
    blocks = nz * 2
    lanes = blocks * 128
    deep = blocks * 128
    pad = padded_columns(width, rows, 64, 0, width)
    pad_half = padded_columns(o_cols, rows, 64, 0, o_cols)
    pick_half = padded_columns(o_cols, rows, 64, k_cols, attn_cols)
    tables = [
        rope_tables(local_rows, start, HD) for start in (y * local_rows, (1 - y) * local_rows)
    ]
    cosine = jnp.concatenate([t[0][:, 0] for t in tables], axis=0)
    sine = jnp.concatenate([t[1][:, 0] for t in tables], axis=0)
    cosine = jnp.concatenate([cosine] * 4, axis=1)
    sine = jnp.concatenate([-sine, sine] * 2, axis=1)
    own_places = y * local_rows + jnp.arange(local_rows, dtype=jnp.int32)
    facing_places = (1 - y) * local_rows + jnp.arange(local_rows, dtype=jnp.int32)
    key_places = jnp.concatenate([own_places, facing_places])
    segment_all = jnp.concatenate([segments_mine, segments_facing])
    allowed = (
        (key_places[None, :] <= own_places[:, None])
        & (segment_all[None, :] == segments_mine[:, None])
    ).astype(f32)
    dims = (nz, rows, width, q_cols, k_cols)
    wide_k = KV * HD + 64
    (w_attn, w_out_wide, gains, first_norm, query, keys, values, probs, attended, middle, second_norm) = (
        run_kernel(
            functools.partial(attention_forward, dims),
            (place, pad, pick_half, mine, facing, allowed, cosine, sine, *attn_own, *attn_other),
            [
                ((2, 2, nz, 2, 128, attn_cols), bf16),
                ((2, deep, lanes // 2), bf16),
                ((8, lanes), f32),
                ((both_rows, lanes), bf16),
                ((local_rows, lanes), bf16),
                ((both_rows, wide_k), bf16),
                ((both_rows, KV * HD), bf16),
                ((KV, groups * local_rows, both_rows), f32),
                ((local_rows, lanes), bf16),
                ((local_rows, lanes), f32),
                ((local_rows, lanes), bf16),
            ],
            [pltpu.VMEM((local_rows, lanes), f32), pltpu.VMEM((both_rows, wide_k), f32)],
        )
    )

    second_got = net.core(second_norm)
    incoming_halves = jnp.stack(jnp.split(incoming_pair, 2, axis=1))
    ff_dims = (nz, ff_rows)
    chip_w = pltpu.VMEM((2, 2, nz, 2, 128, half_ff), bf16)
    gate, upward, mixed, *down_grads = run_kernel(
        functools.partial(feed_forward, ff_dims),
        (place, second_norm, second_got, incoming_halves, *gate_parts, *up_parts),
        [
            ((2, both_rows, half_ff), f32),
            ((2, both_rows, half_ff), f32),
            ((2, both_rows, half_ff), bf16),
            *pack_shapes(nz, ff_rows // 2, o_cols),
        ],
        [chip_w, pltpu.VMEM((2, 2, nz, 2, ff_rows // 2, o_cols), bf16)],
    )
    down_grad = net.reduce(down_grads).reshape(ff_rows, -1)
    out_mine, out_away, back_mine, back_away, *gu_grads = run_kernel(
        functools.partial(feed_backward, ff_dims),
        (place, pad_half, second_norm, second_got, incoming_halves, gate, upward, mixed,
         *gate_parts, *up_parts, *down_parts),
        [
            ((local_rows, lanes), f32),
            ((local_rows, lanes), bf16),
            ((local_rows, lanes), f32),
            ((local_rows, lanes), bf16),
            *pack_shapes(nz, 2, 64, half_ff),
        ],
        [
            chip_w,
            pltpu.VMEM((2, nz, 2, ff_rows, o_cols), bf16),
            pltpu.VMEM((2, 2, nz, 2, 2, 64, half_ff), bf16),
            pltpu.VMEM((both_rows, lanes), f32),
            pltpu.VMEM((both_rows, lanes), f32),
        ],
    )
    gu_sum = net.reduce(gu_grads)
    back_got = net.core(back_away)
    attn_keep, attn_away, grad_middle, first_mine, first_away = run_kernel(
        functools.partial(attention_backward, dims),
        (place, pad, incoming, mine, facing, cosine, sine, back_mine, back_got, w_attn, w_out_wide, gains,
         first_norm, query, keys, values, probs, attended, middle),
        [
            ((8, nz, attn_rows, attn_cols), bf16),
            ((8, nz, attn_rows, attn_cols), bf16),
            ((local_rows, lanes), f32),
            ((local_rows, lanes), f32),
            ((local_rows, lanes), bf16),
        ],
        [
            pltpu.VMEM((local_rows, lanes), f32),
            pltpu.VMEM((both_rows, wide_k), f32),
            pltpu.VMEM((both_rows, KV * HD), f32),
            pltpu.VMEM((local_rows, lanes), bf16),
            pltpu.VMEM((2, 2, 2, nz, 2, attn_rows, attn_cols), bf16),
            pltpu.VMEM((2, both_rows, attn_cols), bf16),
            pltpu.VMEM((2, both_rows, attn_cols), bf16),
            pltpu.VMEM((2, local_rows, attn_cols), bf16),
            pltpu.VMEM((both_rows, lanes), f32),
        ],
    )
    from_core = net.core(attn_away)

    def both_cores(at):
        return (attn_keep[at].astype(f32) + from_core[at].astype(f32)).astype(bf16)

    attn_both = [both_cores(at) for at in (slice(0, 2), slice(2, 4), 4, 5, slice(6, 8))]
    attn_sum = net.reduce(attn_both)

    def narrow(value):
        return value.reshape(local_rows, 2 * blocks, 64)[:, :, :rows].reshape(local_rows, width)

    out_got = net.core(out_away)
    block_output = narrow(middle + out_mine + out_got.astype(f32)).astype(bf16)
    first_got = net.over_y(first_away)
    grad_first = narrow(first_mine + first_got.astype(f32))
    hidden = mine.astype(f32)
    gain = narrow(jnp.broadcast_to(gains[0:1], (local_rows, lanes)))[0]
    _, pull_first = jax.vjp(normed, hidden, gain)
    input_grad = narrow(grad_middle) + pull_first(grad_first)[0]

    def core_rows(total):
        return pick(c, total), net.core(pick(c, (total[1], total[0])).astype(bf16)).astype(f32)

    gu_mine, gu_got = core_rows(gu_sum)

    def columns(which):
        pair = (gu_mine[which, :rows], gu_got[which, :rows])
        parts = (pick(c, pair), pick(c, pair[::-1]))
        starts = range(0, half_ff, ff_rows)
        return jnp.concatenate(
            [part[:, at : at + ff_rows] for at in starts for part in parts], axis=1
        )

    gu_grad = columns(0), columns(1)
    attn_mine, attn_got = (part[:rows] for part in core_rows(attn_sum))
    qk_grad = pick(c, (attn_mine, attn_got))
    vo_grad = pick(c, (attn_got, attn_mine))
    gain_out = attn_sum[0, rows, :256].reshape(2, 2, 64)
    gain_out = pick(c, (gain_out[:, 0, :rows], gain_out[:, 1, :rows]))
    return (
        block_output[None],
        input_grad[None],
        qk_grad[:, :q_cols],
        qk_grad[:, q_cols:],
        vo_grad[:, :k_cols],
        vo_grad[:, k_cols:],
        gu_grad[0],
        gu_grad[1],
        down_grad,
        gain_out,
    )


def fast_body(*args):
    return fast_pass(*args)


def body(
    tokens, segment_ids, norm_gains, w_query, w_key, w_value, w_out, w_gate, w_up, w_down, cotangent
):
    local_rows = tokens.shape[1]
    groups = H // KV
    scale_factor = 1.0 / math.sqrt(HD)
    offset = lax.axis_index("ctx") * local_rows
    column_parts = (
        lax.all_gather(w_query, "ctx", axis=1, tiled=True),
        lax.all_gather(w_key, "ctx", axis=1, tiled=True),
        lax.all_gather(w_value, "ctx", axis=1, tiled=True),
        lax.all_gather(w_out, "ctx", axis=1, tiled=True),
        lax.all_gather(w_gate, "ctx", axis=1, tiled=True),
        lax.all_gather(w_up, "ctx", axis=1, tiled=True),
        lax.all_gather(w_down, "ctx", axis=1, tiled=True),
    )
    forward_set = (
        lax.all_gather(column_parts[0], "dp", axis=0, tiled=True),
        lax.all_gather(column_parts[1], "dp", axis=0, tiled=True),
        lax.all_gather(column_parts[2], "dp", axis=0, tiled=True),
        lax.all_gather(column_parts[3], "dp", axis=0, tiled=True),
        lax.all_gather(column_parts[4], "dp", axis=0, tiled=True),
        lax.all_gather(column_parts[5], "dp", axis=0, tiled=True),
        lax.all_gather(column_parts[6], "dp", axis=0, tiled=True),
        lax.all_gather(norm_gains.astype(jnp.bfloat16), "dp", axis=1, tiled=True).astype(
            norm_gains.dtype
        ),
    )
    query_full, key_full, value_full, out_full, gate_full, up_full, down_full, gains_full = (
        forward_set
    )
    hidden = tokens[0].astype(jnp.float32)
    own_segments = segment_ids[0]
    first_norm = normed(hidden, gains_full[0]).astype(jnp.bfloat16)
    cosine, sine = rope_tables(local_rows, offset, HD)
    query = rotate(matmul(first_norm, query_full).reshape(local_rows, H, HD), cosine, sine).astype(
        jnp.bfloat16
    )
    keys_local = (
        rotate(matmul(first_norm, key_full).reshape(local_rows, KV, HD), cosine, sine)
        .astype(jnp.bfloat16)
        .reshape(local_rows, KV * HD)
    )
    values_local = matmul(first_norm, value_full).astype(jnp.bfloat16)
    key_all, value_all, segment_all = (
        lax.all_gather(keys_local, "ctx", axis=0, tiled=True),
        lax.all_gather(values_local, "ctx", axis=0, tiled=True),
        lax.all_gather(own_segments, "ctx", axis=0, tiled=True),
    )
    length_all = key_all.shape[0]
    key_grid = key_all.reshape(length_all, KV, HD)
    value_grid = value_all.reshape(length_all, KV, HD)
    grouped = query.reshape(local_rows, KV, groups, HD)
    query_places = offset + jnp.arange(local_rows, dtype=jnp.int32)
    key_places = jnp.arange(length_all, dtype=jnp.int32)
    allowed = (key_places[None, :] <= query_places[:, None]) & (
        segment_all[None, :] == own_segments[:, None]
    )
    scores = score_block(grouped, key_grid, scale_factor)
    totals = jnp.sum(jnp.where(allowed, jnp.exp(scores), 0.0), axis=-1, keepdims=True)
    log_total = jnp.log(totals)
    probs = probabilities(scores, allowed, log_total).astype(jnp.bfloat16)
    attended = jnp.einsum("kgts,skd->tkgd", probs, value_grid, preferred_element_type=jnp.float32)
    attended = attended.reshape(local_rows, H * HD).astype(jnp.bfloat16)
    middle = hidden + matmul(attended, out_full)
    second_norm = normed(middle, gains_full[1]).astype(jnp.bfloat16)
    gate = matmul(second_norm, gate_full)
    upward = matmul(second_norm, up_full)
    sigma = jax.nn.sigmoid(gate)
    activated = gate * sigma
    mixed = (activated * upward).astype(jnp.bfloat16)
    block_output = (middle + matmul(mixed, down_full)).astype(jnp.bfloat16)
    query_back, key_back, value_back, out_back, gate_back, up_back, down_back, gains_back = (
        forward_set
    )
    incoming = cotangent[0]
    grad_down = matmul(mixed.T, incoming)
    grad_mixed = matmul(incoming, down_back.T)
    grad_gate = (grad_mixed * upward * sigma * (1.0 + gate * (1.0 - sigma))).astype(jnp.bfloat16)
    grad_upward = (grad_mixed * activated).astype(jnp.bfloat16)
    grad_wgate = matmul(second_norm.T, grad_gate)
    grad_wup = matmul(second_norm.T, grad_upward)
    grad_second = matmul(grad_gate, gate_back.T) + matmul(grad_upward, up_back.T)
    _, pull_second = jax.vjp(normed, middle, gains_back[1])
    grad_middle_norm, grad_gain_second = pull_second(grad_second)
    grad_middle = incoming.astype(jnp.float32) + grad_middle_norm
    grad_branch = grad_middle.astype(jnp.bfloat16)
    grad_wout = matmul(attended.T, grad_branch)
    grad_attended = (
        matmul(grad_branch, out_back.T).astype(jnp.bfloat16).reshape(local_rows, KV, groups, HD)
    )
    exact_probs = probabilities(score_block(grouped, key_grid, scale_factor), allowed, log_total)
    probs_again = exact_probs.astype(jnp.bfloat16)
    grad_values_all = jnp.einsum(
        "kgts,tkgd->skd", probs_again, grad_attended, preferred_element_type=jnp.float32
    )
    grad_probs = jnp.einsum(
        "tkgd,skd->kgts", grad_attended, value_grid, preferred_element_type=jnp.float32
    )
    row_terms = jnp.sum(exact_probs * grad_probs, axis=-1, keepdims=True)
    grad_scores = (exact_probs * (grad_probs - row_terms) * scale_factor).astype(jnp.bfloat16)
    grad_query = jnp.einsum(
        "kgts,skd->tkgd", grad_scores, key_grid, preferred_element_type=jnp.float32
    )
    grad_query = (
        unrotate(grad_query.reshape(local_rows, H, HD), cosine, sine)
        .reshape(local_rows, H * HD)
        .astype(jnp.bfloat16)
    )
    grad_keys_all = jnp.einsum(
        "kgts,tkgd->skd", grad_scores, grouped, preferred_element_type=jnp.float32
    )
    own_keys, own_values = (
        lax.psum_scatter(
            grad_keys_all.reshape(length_all, KV * HD).astype(jnp.bfloat16),
            "ctx",
            scatter_dimension=0,
            tiled=True,
        ).astype(jnp.float32),
        lax.psum_scatter(
            grad_values_all.reshape(length_all, KV * HD).astype(jnp.bfloat16),
            "ctx",
            scatter_dimension=0,
            tiled=True,
        ).astype(jnp.float32),
    )
    grad_keys = (
        unrotate(own_keys.reshape(local_rows, KV, HD), cosine, sine)
        .reshape(local_rows, KV * HD)
        .astype(jnp.bfloat16)
    )
    grad_values = own_values.astype(jnp.bfloat16)
    grad_wquery = matmul(first_norm.T, grad_query)
    grad_wkey = matmul(first_norm.T, grad_keys)
    grad_wvalue = matmul(first_norm.T, grad_values)
    grad_first = (
        matmul(grad_query, query_back.T)
        + matmul(grad_keys, key_back.T)
        + matmul(grad_values, value_back.T)
    )
    _, pull_first = jax.vjp(normed, hidden, gains_back[0])
    grad_hidden_norm, grad_gain_first = pull_first(grad_first)
    input_grad = grad_middle + grad_hidden_norm
    gain_terms = jnp.stack([grad_gain_first, grad_gain_second])
    gain_copies = jnp.broadcast_to(gain_terms[None], (lax.axis_size("ctx"),) + gain_terms.shape)
    by_cols = (
        lax.psum_scatter(
            grad_wquery.astype(jnp.bfloat16), "ctx", scatter_dimension=1, tiled=True
        ).astype(jnp.float32),
        lax.psum_scatter(
            grad_wkey.astype(jnp.bfloat16), "ctx", scatter_dimension=1, tiled=True
        ).astype(jnp.float32),
        lax.psum_scatter(
            grad_wvalue.astype(jnp.bfloat16), "ctx", scatter_dimension=1, tiled=True
        ).astype(jnp.float32),
        lax.psum_scatter(
            grad_wout.astype(jnp.bfloat16), "ctx", scatter_dimension=1, tiled=True
        ).astype(jnp.float32),
        lax.psum_scatter(
            grad_wgate.astype(jnp.bfloat16), "ctx", scatter_dimension=1, tiled=True
        ).astype(jnp.float32),
        lax.psum_scatter(
            grad_wup.astype(jnp.bfloat16), "ctx", scatter_dimension=1, tiled=True
        ).astype(jnp.float32),
        lax.psum_scatter(
            grad_down.astype(jnp.bfloat16), "ctx", scatter_dimension=1, tiled=True
        ).astype(jnp.float32),
        lax.psum_scatter(
            gain_copies.astype(jnp.bfloat16), "ctx", scatter_dimension=0, tiled=True
        ).astype(jnp.float32),
    )
    finals = (
        lax.psum_scatter(
            by_cols[0].astype(jnp.bfloat16), "dp", scatter_dimension=0, tiled=True
        ).astype(jnp.float32),
        lax.psum_scatter(
            by_cols[1].astype(jnp.bfloat16), "dp", scatter_dimension=0, tiled=True
        ).astype(jnp.float32),
        lax.psum_scatter(
            by_cols[2].astype(jnp.bfloat16), "dp", scatter_dimension=0, tiled=True
        ).astype(jnp.float32),
        lax.psum_scatter(
            by_cols[3].astype(jnp.bfloat16), "dp", scatter_dimension=0, tiled=True
        ).astype(jnp.float32),
        lax.psum_scatter(
            by_cols[4].astype(jnp.bfloat16), "dp", scatter_dimension=0, tiled=True
        ).astype(jnp.float32),
        lax.psum_scatter(
            by_cols[5].astype(jnp.bfloat16), "dp", scatter_dimension=0, tiled=True
        ).astype(jnp.float32),
        lax.psum_scatter(
            by_cols[6].astype(jnp.bfloat16), "dp", scatter_dimension=0, tiled=True
        ).astype(jnp.float32),
        lax.psum_scatter(
            by_cols[7].astype(jnp.bfloat16), "dp", scatter_dimension=2, tiled=True
        ).astype(jnp.float32),
    )
    gain_out = finals[7][0]
    return (
        block_output[None],
        input_grad[None],
        finals[0],
        finals[1],
        finals[2],
        finals[3],
        finals[4],
        finals[5],
        finals[6],
        gain_out,
    )


def solution(mesh):
    two_blocks = mesh.shape["ctx"] == 2 and mesh.shape["dp"] % 4 == 0
    return jax.shard_map(
        fast_body if two_blocks else body,
        mesh=mesh,
        in_specs=(
            P("dp", "ctx", None),
            P("dp", "ctx"),
            P(None, "dp"),
            P("dp", "ctx"),
            P("dp", "ctx"),
            P("dp", "ctx"),
            P("dp", "ctx"),
            P("dp", "ctx"),
            P("dp", "ctx"),
            P("dp", "ctx"),
            P("dp", "ctx", None),
        ),
        out_specs=(
            P("dp", "ctx", None),
            P("dp", "ctx", None),
            P("dp", "ctx"),
            P("dp", "ctx"),
            P("dp", "ctx"),
            P("dp", "ctx"),
            P("dp", "ctx"),
            P("dp", "ctx"),
            P("dp", "ctx"),
            P(None, "dp"),
        ),
        check_vma=False,
    )
```

profile of v0, /device:TPU:0, one launch (start us, length us, event | category | flops | bytes accessed | tf_op | source)
XLA Modules:
  0.0 344.7 jit_solution(11348294283862342659)
XLA Ops:
  0.7 5.1 %collective-permute-start.30 = (bf16[2,80,480]{2,1,0:T(8,128)(2,1)}, bf16[2,80,480]{2,1,0:T(8,128)(2,1)S(1)}, u32[]{:S(2)}, u32[]{:S(2)}) collective-permute-start(bf16[2,80,480]{2,1,0:T(8,128)(2,1)} %bitcast.252), channel_id=1, source_target_pairs={{0,24},{1,25},{2,26},{3,27},{4,28},{5,29},{6,30},{7,31},{8,0},{9,1... | collective-permute-start | bytes 460808 | tf_op jit(solution)/shard_map/ppermute | solution.py:95
  11.0 1.6 collective-permute-start
  13.9 2.1 fusion.pad_ref
  20.1 1.6 collective-permute-start.33
  21.7 2.8 collective-permute-start.2
  27.6 2.9 collective-permute-start.23
  32.0 4.4 %collective-permute-start.24 = (bf16[2,64,640]{2,1,0:T(8,128)(2,1)S(1)}, bf16[2,64,640]{2,1,0:T(8,128)(2,1)S(1)}, u32[]{:S(2)}, u32[]{:S(2)}) collective-permute-start(bf16[2,64,640]{2,1,0:T(8,128)(2,1)S(1)} %maximum_select_fusion.2), channel_id=1, source_target_pairs={{0,16},{1,17},{2,18},{3,19},{4,20},{5,21},{6,22},{7,23},{8,24},{9,... | collective-permute-start | bytes 491528 | tf_op jit(solution)/shard_map/ppermute | solution.py:95
  36.4 8.4 %collective-permute-done.3 = bf16[2,64,640]{2,1,0:T(8,128)(2,1)S(1)} collective-permute-done((bf16[2,64,640]{2,1,0:T(8,128)(2,1)S(1)}, bf16[2,64,640]{2,1,0:T(8,128)(2,1)S(1)}, u32[]{:S(2)}, u32[]{:S(2)}) %collective-permute-start.3) | collective-permute-done | bytes 163872 | tf_op jit(solution)/shard_map/ppermute | solution.py:95
  44.8 3.8 %collective-permute-start.16 = (bf16[2,64,640]{2,1,0:T(8,128)(2,1)S(1)}, bf16[2,64,640]{2,1,0:T(8,128)(2,1)S(1)}, u32[]{:S(2)}, u32[]{:S(2)}) collective-permute-start(bf16[2,64,640]{2,1,0:T(8,128)(2,1)S(1)} %maximum_select_fusion.1), channel_id=1, source_target_pairs={{0,24},{1,25},{2,26},{3,27},{4,28},{5,29},{6,30},{7,31},{8,0},{9,1... | collective-permute-start | bytes 491528 | tf_op jit(solution)/shard_map/ppermute | solution.py:95
  48.9 2.7 collective-permute-start.17
  51.6 5.6 %collective-permute-done.24 = bf16[2,64,640]{2,1,0:T(8,128)(2,1)S(1)} collective-permute-done((bf16[2,64,640]{2,1,0:T(8,128)(2,1)S(1)}, bf16[2,64,640]{2,1,0:T(8,128)(2,1)S(1)}, u32[]{:S(2)}, u32[]{:S(2)}) %collective-permute-start.24) | collective-permute-done | bytes 163872 | tf_op jit(solution)/shard_map/ppermute | solution.py:95
  58.9 1.6 collective-permute-start.26
  60.5 8.2 %collective-permute-done.17 = bf16[2,64,640]{2,1,0:T(8,128)(2,1)S(1)} collective-permute-done((bf16[2,64,640]{2,1,0:T(8,128)(2,1)S(1)}, bf16[2,64,640]{2,1,0:T(8,128)(2,1)S(1)}, u32[]{:S(2)}, u32[]{:S(2)}) %collective-permute-start.17) | collective-permute-done | bytes 163872 | tf_op jit(solution)/shard_map/ppermute | solution.py:95
  69.2 1.5 collective-permute-start.6
  73.3 2.4 collective-permute-done.5
  76.2 24.1 %collective-permute-done.6 = bf16[2,4,64,640]{3,2,0,1:T(8,128)(2,1)S(1)} collective-permute-done((bf16[2,4,64,640]{3,2,0,1:T(8,128)(2,1)S(1)}, bf16[2,4,64,640]{3,2,0,1:T(8,128)(2,1)S(1)}, u32[]{:S(2)}, u32[]{:S(2)}) %collective-permute-start.6) | collective-permute-done | bytes 655392 | tf_op jit(solution)/shard_map/ppermute | solution.py:95
  102.3 12.1 %collective-permute-done.20 = bf16[2,4,64,640]{3,2,0,1:T(8,128)(2,1)S(1)} collective-permute-done((bf16[2,4,64,640]{3,2,0,1:T(8,128)(2,1)S(1)}, bf16[2,4,64,640]{3,2,0,1:T(8,128)(2,1)S(1)}, u32[]{:S(2)}, u32[]{:S(2)}) %collective-permute-start.20) | collective-permute-done | bytes 655392 | tf_op jit(solution)/shard_map/ppermute | solution.py:95
  115.7 5.6 %collective-permute-done.7.refs_3_ = bf16[4,64,640]{2,1,0:T(8,128)(2,1)S(1)} collective-permute-done((bf16[4,64,640]{2,1,0:T(8,128)(2,1)S(1)}, bf16[4,64,640]{2,1,0:T(8,128)(2,1)S(1)}, u32[]{:S(2)}, u32[]{:S(2)}) %collective-permute-start.7) | collective-permute-done | bytes 327712 | tf_op jit(solution)/shard_map/ppermute | solution.py:95
  129.0 1.6 collective-permute-start.21
  131.3 1.5 collective-permute-start.22
  132.8 12.8 %shard_map.186 = (bf16[2,2,4,2,128,640]{5,4,3,2,1,0:T(8,128)(2,1)}, bf16[2,1024,512]{2,1,0:T(8,128)(2,1)}, f32[8,1024]{1,0:T(8,128)}, bf16[256,1024]{1,0:T(8,128...) custom-call(s32[3]{0:T(128)} %pad_add_fusion.2.place_ref, ...), custom_call_target="tpu_custom_call" | custom-call | flops 2000000000 | bytes 8749068 | tf_op jit(solution)/shard_map/pallas_call | solution.py:498
  151.4 8.8 %shard_map.187 = (f32[2,256,640]{2,1,0:T(8,128)}, f32[2,256,640]{2,1,0:T(8,128)}, bf16[2,256,640]{2,1,0:T(8,128)(2,1)}, bf16[2,4,80,480]{3,2,1,0:T(8,128)(2,1)},...) custom-call(s32[3]{0:T(128)} %pad_add_fusion.2.place_ref, ...), custom_call_target="tpu_custom_call" | custom-call | flops 2000000000 | bytes 6258700 | tf_op jit(solution)/shard_map/pallas_call | solution.py:498
  160.2 16.2 %shard_map.188 = (f32[128,1024]{1,0:T(8,128)}, bf16[128,1024]{1,0:T(8,128)(2,1)}, f32[128,1024]{1,0:T(8,128)}, bf16[128,1024]{1,0:T(8,128)(2,1)}, bf16[2,4,2,64,...) custom-call(s32[3]{0:T(128)} %pad_add_fusion.2.place_ref, ...), custom_call_target="tpu_custom_call" | custom-call | flops 2000000000 | bytes 12484620 | tf_op jit(solution)/shard_map/pallas_call | solution.py:498
  178.0 1.4 collective-permute-start.57
  179.4 1.5 collective-permute-start.59
  182.3 18.7 %shard_map.189 = (bf16[8,4,64,640]{3,2,1,0:T(8,128)(2,1)}, bf16[8,4,64,640]{3,2,1,0:T(8,128)(2,1)}, f32[128,1024]{1,0:T(8,128)}, f32[128,1024]{1,0:T(8,128)}, bf16[128,1024]{1,0:T(8,128)(2,1)}) custom-call(s32[3]{0:T(128)} %pad_add_fusion.2.place_ref, bf16[960,1024]{1,0:T(8,128)(2,1)} %fusion.pad_ref, bf16[128,960]{1,0:T(8,128)(2,1)} %bitcast.248, ...), custom_call_target="tpu_custom_call" | custom-call | flops 2000000000 | bytes 15024140 | tf_op jit(solution)/shard_map/pallas_call | solution.py:498
  204.5 24.2 %collective-permute-done.39 = bf16[128,1024]{1,0:T(8,128)(2,1)S(1)} collective-permute-done((bf16[128,1024]{1,0:T(8,128)(2,1)}, bf16[128,1024]{1,0:T(8,128)(2,1)S(1)}, u32[]{:S(2)}, u32[]{:S(2)}) %collective-permute-start.39) | collective-permute-done | bytes 262176 | tf_op jit(solution)/shard_map/ppermute | solution.py:95
  231.7 2.0 copy.136
  235.1 1.9 fusion.16
  237.0 1.5 collective-permute-start.58
  238.5 1.8 fusion.15
  241.7 2.1 fusion.5
  244.3 2.1 fusion.4
  247.9 3.3 collective-permute-done.60
  251.2 1.6 fusion.17
  253.2 8.3 %collective-permute-done.50 = bf16[4,2,64,640]{3,2,1,0:T(8,128)(2,1)} collective-permute-done((bf16[4,2,64,640]{3,2,1,0:T(8,128)(2,1)}, bf16[4,2,64,640]{3,2,1,0:T(8,128)(2,1)}, u32[]{:S(2)}, u32[]{:S(2)}) %collective-permute-start.50) | collective-permute-done | bytes 655392 | tf_op jit(solution)/shard_map/ppermute | solution.py:95
  261.5 3.1 collective-permute-done.52
  264.5 2.2 fusion.6
  267.3 4.0 %collective-permute-start.55 = (bf16[2,2,64,640]{3,2,1,0:T(8,128)(2,1)S(1)}, bf16[2,2,64,640]{3,2,1,0:T(8,128)(2,1)S(1)}, u32[]{:S(2)}, u32[]{:S(2)}) collective-permute-start(bf16[2,2,64,640]{3,2,1,0:T(8,128)(2,1)S(1)} %get-tuple-element.84), channel_id=1, source_target_pairs={{0,24},{1,25},{2,26},{3,27},{4,28},{5,29},{6,30},{7,31},{8,0},{9,1... | collective-permute-start | bytes 983048 | tf_op jit(solution)/shard_map/ppermute | solution.py:95
  273.1 6.5 %collective-permute-done.53 = bf16[2,2,64,640]{3,2,1,0:T(8,128)(2,1)S(1)} collective-permute-done((bf16[2,2,64,640]{3,2,1,0:T(8,128)(2,1)S(1)}, bf16[2,2,64,640]{3,2,1,0:T(8,128)(2,1)S(1)}, u32[]{:S(2)}, u32[]{:S(2)}) %collective-permute-start.53) | collective-permute-done | bytes 327712 | tf_op jit(solution)/shard_map/ppermute | solution.py:95
  279.6 12.5 %collective-permute-done.54 = bf16[2,2,64,640]{3,2,1,0:T(8,128)(2,1)S(1)} collective-permute-done((bf16[2,2,64,640]{3,2,1,0:T(8,128)(2,1)S(1)}, bf16[2,2,64,640]{3,2,1,0:T(8,128)(2,1)S(1)}, u32[]{:S(2)}, u32[]{:S(2)}) %collective-permute-start.54) | collective-permute-done | bytes 327712 | tf_op jit(solution)/shard_map/ppermute | solution.py:95
  292.4 1.4 copy-done.4
  293.9 1.5 add_convert_fusion
  297.5 13.5 %collective-permute-done.41 = bf16[2,4,64,640]{3,2,1,0:T(8,128)(2,1)S(1)} collective-permute-done((bf16[2,4,64,640]{3,2,1,0:T(8,128)(2,1)S(1)}, bf16[2,4,64,640]{3,2,1,0:T(8,128)(2,1)S(1)}, u32[]{:S(2)}, u32[]{:S(2)}) %collective-permute-start.41) | collective-permute-done | bytes 655392 | tf_op jit(solution)/shard_map/ppermute | solution.py:95
  315.6 5.5 %collective-permute-done.42 = bf16[4,64,640]{2,1,0:T(8,128)(2,1)S(1)} collective-permute-done((bf16[4,64,640]{2,1,0:T(8,128)(2,1)}, bf16[4,64,640]{2,1,0:T(8,128)(2,1)S(1)}, u32[]{:S(2)}, u32[]{:S(2)}) %collective-permute-start.42) | collective-permute-done | bytes 327712 | tf_op jit(solution)/shard_map/ppermute | solution.py:95
  323.5 7.0 %collective-permute-start.45 = (bf16[2,64,640]{2,1,0:T(8,128)(2,1)S(1)}, bf16[2,64,640]{2,1,0:T(8,128)(2,1)S(1)}, u32[]{:S(2)}, u32[]{:S(2)}) collective-permute-start(bf16[2,64,640]{2,1,0:T(8,128)(2,1)S(1)} %get-tuple-element.97), channel_id=1, source_target_pairs={{0,8},{1,9},{2,10},{3,11},{4,12},{5,13},{6,14},{7,15},{8,16},{9,17... | collective-permute-start | bytes 491528 | tf_op jit(solution)/shard_map/ppermute | solution.py:95
  330.7 2.3 collective-permute-start.47
  335.3 5.1 %collective-permute-done.46 = bf16[2,64,640]{2,1,0:T(8,128)(2,1)S(1)} collective-permute-done((bf16[2,64,640]{2,1,0:T(8,128)(2,1)S(1)}, bf16[2,64,640]{2,1,0:T(8,128)(2,1)S(1)}, u32[]{:S(2)}, u32[]{:S(2)}) %collective-permute-start.46) | collective-permute-done | bytes 163872 | tf_op jit(solution)/shard_map/ppermute | solution.py:95
  (301 shorter events, 70.5 us)
Async XLA Ops:
  0.7 19.2 %collective-permute-start.30 = (bf16[2,80,480]{2,1,0:T(8,128)(2,1)}, bf16[2,80,480]{2,1,0:T(8,128)(2,1)S(1)}, u32[]{:S(2)}, u32[]{:S(2)}) collective-permute-start(bf16[2,80,480]{2,1,0:T(8,128)(2,1)} %bitcast.252), channel_id=1, source_target_pairs={{0,24},{1,25},{2,26},{3,27},{4,28},{5,29},{6,30},{7,31},{8,0},{9,1... | collective-permute-start | bytes 460808 | tf_op jit(solution)/shard_map/ppermute | solution.py:95
  5.8 14.1 %collective-permute-start.31 = (bf16[2,80,480]{2,1,0:T(8,128)(2,1)}, bf16[2,80,480]{2,1,0:T(8,128)(2,1)S(1)}, u32[]{:S(2)}, u32[]{:S(2)}) collective-permute-start(bf16[2,80,480]{2,1,0:T(8,128)(2,1)} %bitcast.253), channel_id=1, source_target_pairs={{0,16},{1,17},{2,18},{3,19},{4,20},{5,21},{6,22},{7,23},{8,24},{9,... | collective-permute-start | bytes 460808 | tf_op jit(solution)/shard_map/ppermute | solution.py:95
  5.8 14.1 %collective-permute-start.32 = (bf16[2,80,480]{2,1,0:T(8,128)(2,1)}, bf16[2,80,480]{2,1,0:T(8,128)(2,1)S(1)}, u32[]{:S(2)}, u32[]{:S(2)}) collective-permute-start(bf16[2,80,480]{2,1,0:T(8,128)(2,1)} %bitcast.254), channel_id=1, source_target_pairs={{0,8},{1,9},{2,10},{3,11},{4,12},{5,13},{6,14},{7,15},{8,16},{9,17... | collective-permute-start | bytes 460808 | tf_op jit(solution)/shard_map/ppermute | solution.py:95
  11.0 16.6 %collective-permute-start = (bf16[136,960]{1,0:T(8,128)(2,1)S(1)}, bf16[136,960]{1,0:T(8,128)(2,1)S(1)}, u32[]{:S(2)}, u32[]{:S(2)}) collective-permute-start(bf16[136,960]{1,0:T(8,128)(2,1)S(1)} %fusion.37), channel_id=1, source_target_pairs={{0,1},{1,0},{2,3},{3,2},{4,5},{5,4},{6,7},{7,6},{8,9},{9,8},{10,11... | collective-permute-start | bytes 783368 | tf_op jit(solution)/shard_map/ppermute | solution.py:95
  20.1 51.8 %collective-permute-start.33 = (bf16[2,4,80,480]{3,2,1,0:T(8,128)(2,1)S(1)}, bf16[2,4,80,480]{3,2,1,0:T(8,128)(2,1)S(1)}, u32[]{:S(2)}, u32[]{:S(2)}) collective-permute-start(bf16[2,4,80,480]{3,2,1,0:T(8,128)(2,1)S(1)} %pad_maximum_fusion.6.refs_10_), channel_id=1, source_target_pairs={{0,4},{1,5},{2,6},{3,7},{4,0},{5,1},{6,2},{7,3},{8,12},{9,13},{10,... | collective-permute-start | bytes 1843208 | tf_op jit(solution)/shard_map/ppermute | solution.py:95
  24.6 20.2 %collective-permute-start.3 = (bf16[2,64,640]{2,1,0:T(8,128)(2,1)S(1)}, bf16[2,64,640]{2,1,0:T(8,128)(2,1)S(1)}, u32[]{:S(2)}, u32[]{:S(2)}) collective-permute-start(bf16[2,64,640]{2,1,0:T(8,128)(2,1)S(1)} %maximum_select_fusion), channel_id=1, source_target_pairs={{0,16},{1,17},{2,18},{3,19},{4,20},{5,21},{6,22},{7,23},{8,24},{9,... | collective-permute-start | bytes 491528 | tf_op jit(solution)/shard_map/ppermute | solution.py:95
  25.8 19.0 %collective-permute-start.4 = (bf16[2,64,640]{2,1,0:T(8,128)(2,1)S(1)}, bf16[2,64,640]{2,1,0:T(8,128)(2,1)S(1)}, u32[]{:S(2)}, u32[]{:S(2)}) collective-permute-start(bf16[2,64,640]{2,1,0:T(8,128)(2,1)S(1)} %maximum_select_fusion), channel_id=1, source_target_pairs={{0,8},{1,9},{2,10},{3,11},{4,12},{5,13},{6,14},{7,15},{8,16},{9,17... | collective-permute-start | bytes 491528 | tf_op jit(solution)/shard_map/ppermute | solution.py:95
  27.6 21.2 %collective-permute-start.23 = (bf16[2,64,640]{2,1,0:T(8,128)(2,1)S(1)}, bf16[2,64,640]{2,1,0:T(8,128)(2,1)S(1)}, u32[]{:S(2)}, u32[]{:S(2)}) collective-permute-start(bf16[2,64,640]{2,1,0:T(8,128)(2,1)S(1)} %maximum_select_fusion.2), channel_id=1, source_target_pairs={{0,24},{1,25},{2,26},{3,27},{4,28},{5,29},{6,30},{7,31},{8,0},{9,1... | collective-permute-start | bytes 491528 | tf_op jit(solution)/shard_map/ppermute | solution.py:95
  32.0 25.1 %collective-permute-start.24 = (bf16[2,64,640]{2,1,0:T(8,128)(2,1)S(1)}, bf16[2,64,640]{2,1,0:T(8,128)(2,1)S(1)}, u32[]{:S(2)}, u32[]{:S(2)}) collective-permute-start(bf16[2,64,640]{2,1,0:T(8,128)(2,1)S(1)} %maximum_select_fusion.2), channel_id=1, source_target_pairs={{0,16},{1,17},{2,18},{3,19},{4,20},{5,21},{6,22},{7,23},{8,24},{9,... | collective-permute-start | bytes 491528 | tf_op jit(solution)/shard_map/ppermute | solution.py:95
  44.8 13.3 %collective-permute-start.25 = (bf16[2,64,640]{2,1,0:T(8,128)(2,1)S(1)}, bf16[2,64,640]{2,1,0:T(8,128)(2,1)S(1)}, u32[]{:S(2)}, u32[]{:S(2)}) collective-permute-start(bf16[2,64,640]{2,1,0:T(8,128)(2,1)S(1)} %maximum_select_fusion.2), channel_id=1, source_target_pairs={{0,8},{1,9},{2,10},{3,11},{4,12},{5,13},{6,14},{7,15},{8,16},{9,17... | collective-permute-start | bytes 491528 | tf_op jit(solution)/shard_map/ppermute | solution.py:95
  44.8 14.1 %collective-permute-start.16 = (bf16[2,64,640]{2,1,0:T(8,128)(2,1)S(1)}, bf16[2,64,640]{2,1,0:T(8,128)(2,1)S(1)}, u32[]{:S(2)}, u32[]{:S(2)}) collective-permute-start(bf16[2,64,640]{2,1,0:T(8,128)(2,1)S(1)} %maximum_select_fusion.1), channel_id=1, source_target_pairs={{0,24},{1,25},{2,26},{3,27},{4,28},{5,29},{6,30},{7,31},{8,0},{9,1... | collective-permute-start | bytes 491528 | tf_op jit(solution)/shard_map/ppermute | solution.py:95
  48.9 19.8 %collective-permute-start.17 = (bf16[2,64,640]{2,1,0:T(8,128)(2,1)S(1)}, bf16[2,64,640]{2,1,0:T(8,128)(2,1)S(1)}, u32[]{:S(2)}, u32[]{:S(2)}) collective-permute-start(bf16[2,64,640]{2,1,0:T(8,128)(2,1)S(1)} %maximum_select_fusion.1), channel_id=1, source_target_pairs={{0,16},{1,17},{2,18},{3,19},{4,20},{5,21},{6,22},{7,23},{8,24},{9,... | collective-permute-start | bytes 491528 | tf_op jit(solution)/shard_map/ppermute | solution.py:95
  57.1 12.1 %collective-permute-start.18 = (bf16[2,64,640]{2,1,0:T(8,128)(2,1)S(1)}, bf16[2,64,640]{2,1,0:T(8,128)(2,1)S(1)}, u32[]{:S(2)}, u32[]{:S(2)}) collective-permute-start(bf16[2,64,640]{2,1,0:T(8,128)(2,1)S(1)} %maximum_select_fusion.1), channel_id=1, source_target_pairs={{0,8},{1,9},{2,10},{3,11},{4,12},{5,13},{6,14},{7,15},{8,16},{9,17... | collective-permute-start | bytes 491528 | tf_op jit(solution)/shard_map/ppermute | solution.py:95
  58.1 17.6 %collective-permute-start.5 = (bf16[2,4,64,640]{3,2,0,1:T(8,128)(2,1)S(1)}, bf16[2,4,64,640]{3,2,0,1:T(8,128)(2,1)S(1)}, u32[]{:S(2)}, u32[]{:S(2)}) collective-permute-start(bf16[2,4,64,640]{3,2,0,1:T(8,128)(2,1)S(1)} %pad_maximum_fusion.3), channel_id=1, source_target_pairs={{0,4},{1,5},{2,6},{3,7},{4,0},{5,1},{6,2},{7,3},{8,12},{9,13},{10,... | collective-permute-start | bytes 1966088 | tf_op jit(solution)/shard_map/ppermute | solution.py:95
  58.9 41.4 %collective-permute-start.26 = (bf16[2,4,64,640]{3,2,1,0:T(8,128)(2,1)S(1)}, bf16[2,4,64,640]{3,2,1,0:T(8,128)(2,1)S(1)}, u32[]{:S(2)}, u32[]{:S(2)}) collective-permute-start(bf16[2,4,64,640]{3,2,1,0:T(8,128)(2,1)S(1)} %pad_maximum_fusion.5.refs_5_), channel_id=1, source_target_pairs={{0,4},{1,5},{2,6},{3,7},{4,0},{5,1},{6,2},{7,3},{8,12},{9,13},{10,... | collective-permute-start | bytes 1966088 | tf_op jit(solution)/shard_map/ppermute | solution.py:95
  68.7 32.3 %collective-permute-start.27 = (bf16[2,4,64,640]{3,2,1,0:T(8,128)(2,1)S(1)}, bf16[2,4,64,640]{3,2,1,0:T(8,128)(2,1)S(1)}, u32[]{:S(2)}, u32[]{:S(2)}) collective-permute-start(bf16[2,4,64,640]{3,2,1,0:T(8,128)(2,1)S(1)} %pad_maximum_fusion.5.refs_5_), channel_id=1, source_target_pairs={{0,1},{1,0},{2,3},{3,2},{4,5},{5,4},{6,7},{7,6},{8,9},{9,8},{10,11... | collective-permute-start | bytes 1966088 | tf_op jit(solution)/shard_map/ppermute | solution.py:95
  69.2 31.1 %collective-permute-start.6 = (bf16[2,4,64,640]{3,2,0,1:T(8,128)(2,1)S(1)}, bf16[2,4,64,640]{3,2,0,1:T(8,128)(2,1)S(1)}, u32[]{:S(2)}, u32[]{:S(2)}) collective-permute-start(bf16[2,4,64,640]{3,2,0,1:T(8,128)(2,1)S(1)} %pad_maximum_fusion.3), channel_id=1, source_target_pairs={{0,1},{1,0},{2,3},{3,2},{4,5},{5,4},{6,7},{7,6},{8,9},{9,8},{10,11... | collective-permute-start | bytes 1966088 | tf_op jit(solution)/shard_map/ppermute | solution.py:95
  71.9 30.3 %collective-permute-start.19 = (bf16[2,4,64,640]{3,2,0,1:T(8,128)(2,1)S(1)}, bf16[2,4,64,640]{3,2,0,1:T(8,128)(2,1)S(1)}, u32[]{:S(2)}, u32[]{:S(2)}) collective-permute-start(bf16[2,4,64,640]{3,2,0,1:T(8,128)(2,1)S(1)} %pad_maximum_fusion.4), channel_id=1, source_target_pairs={{0,4},{1,5},{2,6},{3,7},{4,0},{5,1},{6,2},{7,3},{8,12},{9,13},{10,... | collective-permute-start | bytes 1966088 | tf_op jit(solution)/shard_map/ppermute | solution.py:95
  75.7 38.6 %collective-permute-start.20 = (bf16[2,4,64,640]{3,2,0,1:T(8,128)(2,1)S(1)}, bf16[2,4,64,640]{3,2,0,1:T(8,128)(2,1)S(1)}, u32[]{:S(2)}, u32[]{:S(2)}) collective-permute-start(bf16[2,4,64,640]{3,2,0,1:T(8,128)(2,1)S(1)} %pad_maximum_fusion.4), channel_id=1, source_target_pairs={{0,1},{1,0},{2,3},{3,2},{4,5},{5,4},{6,7},{7,6},{8,9},{9,8},{10,11... | collective-permute-start | bytes 1966088 | tf_op jit(solution)/shard_map/ppermute | solution.py:95
  100.3 14.9 %collective-permute-start.9 = (bf16[2,4,64,640]{3,2,0,1:T(8,128)(2,1)S(1)}, bf16[2,4,64,640]{3,2,0,1:T(8,128)(2,1)S(1)}, u32[]{:S(2)}, u32[]{:S(2)}) collective-permute-start(bf16[2,4,64,640]{3,2,0,1:T(8,128)(2,1)S(1)} %pad_maximum_fusion.3), channel_id=1, source_target_pairs={{0,2},{1,3},{2,0},{3,1},{4,6},{5,7},{6,4},{7,5},{8,10},{9,11},{10,... | collective-permute-start | bytes 1966088 | tf_op jit(solution)/shard_map/ppermute | solution.py:95
  100.4 20.9 %collective-permute-start.7 = (bf16[4,64,640]{2,1,0:T(8,128)(2,1)S(1)}, bf16[4,64,640]{2,1,0:T(8,128)(2,1)S(1)}, u32[]{:S(2)}, u32[]{:S(2)}) collective-permute-start(bf16[4,64,640]{2,1,0:T(8,128)(2,1)S(1)} %slice_bitcast_fusion.11), channel_id=1, source_target_pairs={{0,1},{1,0},{2,3},{3,2},{4,5},{5,4},{6,7},{7,6},{8,9},{9,8},{10,11... | collective-permute-start | bytes 983048 | tf_op jit(solution)/shard_map/ppermute | solution.py:95
  100.9 20.4 %collective-permute-start.8 = (bf16[4,64,640]{2,1,0:T(8,128)(2,1)S(1)}, bf16[4,64,640]{2,1,0:T(8,128)(2,1)S(1)}, u32[]{:S(2)}, u32[]{:S(2)}) collective-permute-start(bf16[4,64,640]{2,1,0:T(8,128)(2,1)S(1)} %slice_bitcast_fusion.10), channel_id=1, source_target_pairs={{0,4},{1,5},{2,6},{3,7},{4,0},{5,1},{6,2},{7,3},{8,12},{9,13},{10,... | collective-permute-start | bytes 983048 | tf_op jit(solution)/shard_map/ppermute | solution.py:95
  102.3 23.8 %collective-permute-start.10 = (bf16[2,4,64,640]{3,2,0,1:T(8,128)(2,1)S(1)}, bf16[2,4,64,640]{3,2,0,1:T(8,128)(2,1)S(1)}, u32[]{:S(2)}, u32[]{:S(2)}) collective-permute-start(bf16[2,4,64,640]{3,2,0,1:T(8,128)(2,1)S(1)} %collective-permute-done.5), channel_id=1, source_target_pairs={{0,2},{1,3},{2,0},{3,1},{4,6},{5,7},{6,4},{7,5},{8,10},{9,11},{10,... | collective-permute-start | bytes 1966088 | tf_op jit(solution)/shard_map/ppermute | solution.py:95
  114.3 13.2 %collective-permute-start.11 = (bf16[2,4,64,640]{3,2,0,1:T(8,128)(2,1)S(1)}, bf16[2,4,64,640]{3,2,0,1:T(8,128)(2,1)S(1)}, u32[]{:S(2)}, u32[]{:S(2)}) collective-permute-start(bf16[2,4,64,640]{3,2,0,1:T(8,128)(2,1)S(1)} %collective-permute-done.6), channel_id=1, source_target_pairs={{0,2},{1,3},{2,0},{3,1},{4,6},{5,7},{6,4},{7,5},{8,10},{9,11},{10,... | collective-permute-start | bytes 1966088 | tf_op jit(solution)/shard_map/ppermute | solution.py:95
  115.2 30.4 %collective-permute-start.34 = (bf16[2,4,80,480]{3,2,1,0:T(8,128)(2,1)S(1)}, bf16[2,4,80,480]{3,2,1,0:T(8,128)(2,1)S(1)}, u32[]{:S(2)}, u32[]{:S(2)}) collective-permute-start(bf16[2,4,80,480]{3,2,1,0:T(8,128)(2,1)S(1)} %pad_maximum_fusion.6.refs_10_), channel_id=1, source_target_pairs={{0,1},{1,0},{2,3},{3,2},{4,5},{5,4},{6,7},{7,6},{8,9},{9,8},{10,11... | collective-permute-start | bytes 1843208 | tf_op jit(solution)/shard_map/ppermute | solution.py:95
  126.1 20.4 %collective-permute-start.28 = (bf16[4,64,640]{2,1,0:T(8,128)(2,1)}, bf16[4,64,640]{2,1,0:T(8,128)(2,1)S(1)}, u32[]{:S(2)}, u32[]{:S(2)}) collective-permute-start(bf16[4,64,640]{2,1,0:T(8,128)(2,1)} %slice_bitcast_fusion.7), channel_id=1, source_target_pairs={{0,1},{1,0},{2,3},{3,2},{4,5},{5,4},{6,7},{7,6},{8,9},{9,8},{10,11... | collective-permute-start | bytes 983048 | tf_op jit(solution)/shard_map/ppermute | solution.py:95
  127.5 19.7 %collective-permute-start.29 = (bf16[4,64,640]{2,1,0:T(8,128)(2,1)}, bf16[4,64,640]{2,1,0:T(8,128)(2,1)S(1)}, u32[]{:S(2)}, u32[]{:S(2)}) collective-permute-start(bf16[4,64,640]{2,1,0:T(8,128)(2,1)} %slice_bitcast_fusion.6), channel_id=1, source_target_pairs={{0,4},{1,5},{2,6},{3,7},{4,0},{5,1},{6,2},{7,3},{8,12},{9,13},{10,... | collective-permute-start | bytes 983048 | tf_op jit(solution)/shard_map/ppermute | solution.py:95
  129.0 22.4 %collective-permute-start.21 = (bf16[4,64,640]{2,1,0:T(8,128)(2,1)}, bf16[4,64,640]{2,1,0:T(8,128)(2,1)}, u32[]{:S(2)}, u32[]{:S(2)}) collective-permute-start(bf16[4,64,640]{2,1,0:T(8,128)(2,1)} %slice_bitcast_fusion.9), channel_id=1, source_target_pairs={{0,1},{1,0},{2,3},{3,2},{4,5},{5,4},{6,7},{7,6},{8,9},{9,8},{10,11... | collective-permute-start | bytes 983048 | tf_op jit(solution)/shard_map/ppermute | solution.py:95
  131.3 20.1 %collective-permute-start.22 = (bf16[4,64,640]{2,1,0:T(8,128)(2,1)}, bf16[4,64,640]{2,1,0:T(8,128)(2,1)}, u32[]{:S(2)}, u32[]{:S(2)}) collective-permute-start(bf16[4,64,640]{2,1,0:T(8,128)(2,1)} %slice_bitcast_fusion.8), channel_id=1, source_target_pairs={{0,4},{1,5},{2,6},{3,7},{4,0},{5,1},{6,2},{7,3},{8,12},{9,13},{10,... | collective-permute-start | bytes 983048 | tf_op jit(solution)/shard_map/ppermute | solution.py:95
  146.5 13.7 %collective-permute-start.35 = (bf16[4,80,480]{2,1,0:T(8,128)(2,1)}, bf16[4,80,480]{2,1,0:T(8,128)(2,1)}, u32[]{:S(2)}, u32[]{:S(2)}) collective-permute-start(bf16[4,80,480]{2,1,0:T(8,128)(2,1)} %slice_bitcast_fusion.5), channel_id=1, source_target_pairs={{0,1},{1,0},{2,3},{3,2},{4,5},{5,4},{6,7},{7,6},{8,9},{9,8},{10,11... | collective-permute-start | bytes 921608 | tf_op jit(solution)/shard_map/ppermute | solution.py:95
  147.2 13.0 %collective-permute-start.36 = (bf16[4,80,480]{2,1,0:T(8,128)(2,1)}, bf16[4,80,480]{2,1,0:T(8,128)(2,1)}, u32[]{:S(2)}, u32[]{:S(2)}) collective-permute-start(bf16[4,80,480]{2,1,0:T(8,128)(2,1)} %slice_bitcast_fusion.4), channel_id=1, source_target_pairs={{0,4},{1,5},{2,6},{3,7},{4,0},{5,1},{6,2},{7,3},{8,12},{9,13},{10,... | collective-permute-start | bytes 921608 | tf_op jit(solution)/shard_map/ppermute | solution.py:95
  176.6 24.4 %collective-permute-start.37 = (bf16[128,1024]{1,0:T(8,128)(2,1)}, bf16[128,1024]{1,0:T(8,128)(2,1)S(1)}, u32[]{:S(2)}, u32[]{:S(2)}) collective-permute-start(bf16[128,1024]{1,0:T(8,128)(2,1)} %get-tuple-element.49), channel_id=1, source_target_pairs={{0,2},{1,3},{2,0},{3,1},{4,6},{5,7},{6,4},{7,5},{8,10},{9,11},{10,... | collective-permute-start | bytes 786440 | tf_op jit(solution)/shard_map/ppermute | solution.py:95
  178.0 57.1 %collective-permute-start.57 = (bf16[2,4,80,480]{3,2,1,0:T(8,128)(2,1)}, bf16[2,4,80,480]{3,2,1,0:T(8,128)(2,1)}, u32[]{:S(2)}, u32[]{:S(2)}) collective-permute-start(bf16[2,4,80,480]{3,2,1,0:T(8,128)(2,1)} %get-tuple-element.72), channel_id=1, source_target_pairs={{0,1},{1,0},{2,3},{3,2},{4,5},{5,4},{6,7},{7,6},{8,9},{9,8},{10,11... | collective-permute-start | bytes 1843208 | tf_op jit(solution)/shard_map/ppermute | solution.py:95
  179.4 59.1 %collective-permute-start.59 = (bf16[2,4,80,480]{3,2,1,0:T(8,128)(2,1)}, bf16[2,4,80,480]{3,2,1,0:T(8,128)(2,1)}, u32[]{:S(2)}, u32[]{:S(2)}) collective-permute-start(bf16[2,4,80,480]{3,2,1,0:T(8,128)(2,1)} %get-tuple-element.74), channel_id=1, source_target_pairs={{0,4},{1,5},{2,6},{3,7},{4,0},{5,1},{6,2},{7,3},{8,12},{9,13},{10,... | collective-permute-start | bytes 1843208 | tf_op jit(solution)/shard_map/ppermute | solution.py:95
  180.9 60.8 %collective-permute-start.49 = (bf16[2,4,2,64,640]{4,3,2,1,0:T(8,128)(2,1)}, bf16[2,4,2,64,640]{4,3,2,1,0:T(8,128)(2,1)}, u32[]{:S(2)}, u32[]{:S(2)}) collective-permute-start(bf16[2,4,2,64,640]{4,3,2,1,0:T(8,128)(2,1)} %get-tuple-element.67), channel_id=1, source_target_pairs={{0,1},{1,0},{2,3},{3,2},{4,5},{5,4},{6,7},{7,6},{8,9},{9,8},{10,11... | collective-permute-start | bytes 3932168 | tf_op jit(solution)/shard_map/ppermute | solution.py:95
  181.6 62.8 %collective-permute-start.51 = (bf16[2,4,2,64,640]{4,3,2,1,0:T(8,128)(2,1)}, bf16[2,4,2,64,640]{4,3,2,1,0:T(8,128)(2,1)}, u32[]{:S(2)}, u32[]{:S(2)}) collective-permute-start(bf16[2,4,2,64,640]{4,3,2,1,0:T(8,128)(2,1)} %get-tuple-element.69), channel_id=1, source_target_pairs={{0,4},{1,5},{2,6},{3,7},{4,0},{5,1},{6,2},{7,3},{8,12},{9,13},{10,... | collective-permute-start | bytes 3932168 | tf_op jit(solution)/shard_map/ppermute | solution.py:95
  201.0 27.7 %collective-permute-start.39 = (bf16[128,1024]{1,0:T(8,128)(2,1)}, bf16[128,1024]{1,0:T(8,128)(2,1)S(1)}, u32[]{:S(2)}, u32[]{:S(2)}) collective-permute-start(bf16[128,1024]{1,0:T(8,128)(2,1)} %get-tuple-element.63), channel_id=1, source_target_pairs={{0,1},{1,0},{2,3},{3,2},{4,5},{5,4},{6,7},{7,6},{8,9},{9,8},{10,11... | collective-permute-start | bytes 786440 | tf_op jit(solution)/shard_map/ppermute | solution.py:95
  228.7 63.7 %collective-permute-start.40 = (bf16[8,4,64,640]{3,2,1,0:T(8,128)(2,1)}, bf16[8,4,64,640]{3,2,1,0:T(8,128)(2,1)S(1)}, u32[]{:S(2)}, u32[]{:S(2)}) collective-permute-start(bf16[8,4,64,640]{3,2,1,0:T(8,128)(2,1)} %get-tuple-element.65), channel_id=1, source_target_pairs={{0,2},{1,3},{2,0},{3,1},{4,6},{5,7},{6,4},{7,5},{8,10},{9,11},{10,... | collective-permute-start | bytes 7864328 | tf_op jit(solution)/shard_map/ppermute | solution.py:95
  243.8 17.7 %collective-permute-start.50 = (bf16[4,2,64,640]{3,2,1,0:T(8,128)(2,1)}, bf16[4,2,64,640]{3,2,1,0:T(8,128)(2,1)}, u32[]{:S(2)}, u32[]{:S(2)}) collective-permute-start(bf16[4,2,64,640]{3,2,1,0:T(8,128)(2,1)} %fusion.5), channel_id=1, source_target_pairs={{0,4},{1,5},{2,6},{3,7},{4,0},{5,1},{6,2},{7,3},{8,12},{9,13},{10,... | collective-permute-start | bytes 1966088 | tf_op jit(solution)/shard_map/ppermute | solution.py:95
  246.5 18.1 %collective-permute-start.52 = (bf16[4,2,64,640]{3,2,1,0:T(8,128)(2,1)}, bf16[4,2,64,640]{3,2,1,0:T(8,128)(2,1)}, u32[]{:S(2)}, u32[]{:S(2)}) collective-permute-start(bf16[4,2,64,640]{3,2,1,0:T(8,128)(2,1)} %fusion.4), channel_id=1, source_target_pairs={{0,1},{1,0},{2,3},{3,2},{4,5},{5,4},{6,7},{7,6},{8,9},{9,8},{10,11... | collective-permute-start | bytes 1966088 | tf_op jit(solution)/shard_map/ppermute | solution.py:95
  253.0 14.2 %collective-permute-start.61 = (bf16[2,80,480]{2,1,0:T(8,128)(2,1)S(1)}, bf16[2,80,480]{2,1,0:T(8,128)(2,1)S(1)}, u32[]{:S(2)}, u32[]{:S(2)}) collective-permute-start(bf16[2,80,480]{2,1,0:T(8,128)(2,1)S(1)} %get-tuple-element.88), channel_id=1, source_target_pairs={{0,8},{1,9},{2,10},{3,11},{4,12},{5,13},{6,14},{7,15},{8,16},{9,17... | collective-permute-start | bytes 460808 | tf_op jit(solution)/shard_map/ppermute | solution.py:95
  253.1 14.2 %collective-permute-start.62 = (bf16[2,80,480]{2,1,0:T(8,128)(2,1)S(1)}, bf16[2,80,480]{2,1,0:T(8,128)(2,1)S(1)}, u32[]{:S(2)}, u32[]{:S(2)}) collective-permute-start(bf16[2,80,480]{2,1,0:T(8,128)(2,1)S(1)} %get-tuple-element.90), channel_id=1, source_target_pairs={{0,16},{1,17},{2,18},{3,19},{4,20},{5,21},{6,22},{7,23},{8,24},{9,... | collective-permute-start | bytes 460808 | tf_op jit(solution)/shard_map/ppermute | solution.py:95
  267.1 12.5 %collective-permute-start.53 = (bf16[2,2,64,640]{3,2,1,0:T(8,128)(2,1)S(1)}, bf16[2,2,64,640]{3,2,1,0:T(8,128)(2,1)S(1)}, u32[]{:S(2)}, u32[]{:S(2)}) collective-permute-start(bf16[2,2,64,640]{3,2,1,0:T(8,128)(2,1)S(1)} %get-tuple-element.83), channel_id=1, source_target_pairs={{0,8},{1,9},{2,10},{3,11},{4,12},{5,13},{6,14},{7,15},{8,16},{9,17... | collective-permute-start | bytes 983048 | tf_op jit(solution)/shard_map/ppermute | solution.py:95
  267.2 24.9 %collective-permute-start.54 = (bf16[2,2,64,640]{3,2,1,0:T(8,128)(2,1)S(1)}, bf16[2,2,64,640]{3,2,1,0:T(8,128)(2,1)S(1)}, u32[]{:S(2)}, u32[]{:S(2)}) collective-permute-start(bf16[2,2,64,640]{3,2,1,0:T(8,128)(2,1)S(1)} %get-tuple-element.85), channel_id=1, source_target_pairs={{0,16},{1,17},{2,18},{3,19},{4,20},{5,21},{6,22},{7,23},{8,24},{9,... | collective-permute-start | bytes 983048 | tf_op jit(solution)/shard_map/ppermute | solution.py:95
  267.3 24.9 %collective-permute-start.55 = (bf16[2,2,64,640]{3,2,1,0:T(8,128)(2,1)S(1)}, bf16[2,2,64,640]{3,2,1,0:T(8,128)(2,1)S(1)}, u32[]{:S(2)}, u32[]{:S(2)}) collective-permute-start(bf16[2,2,64,640]{3,2,1,0:T(8,128)(2,1)S(1)} %get-tuple-element.84), channel_id=1, source_target_pairs={{0,24},{1,25},{2,26},{3,27},{4,28},{5,29},{6,30},{7,31},{8,0},{9,1... | collective-permute-start | bytes 983048 | tf_op jit(solution)/shard_map/ppermute | solution.py:95
  295.3 15.7 %collective-permute-start.41 = (bf16[2,4,64,640]{3,2,1,0:T(8,128)(2,1)S(1)}, bf16[2,4,64,640]{3,2,1,0:T(8,128)(2,1)S(1)}, u32[]{:S(2)}, u32[]{:S(2)}) collective-permute-start(bf16[2,4,64,640]{3,2,1,0:T(8,128)(2,1)S(1)} %get-tuple-element.81), channel_id=1, source_target_pairs={{0,1},{1,0},{2,3},{3,2},{4,5},{5,4},{6,7},{7,6},{8,9},{9,8},{10,11... | collective-permute-start | bytes 1966088 | tf_op jit(solution)/shard_map/ppermute | solution.py:95
  296.7 15.4 %collective-permute-start.43 = (bf16[2,4,64,640]{3,2,1,0:T(8,128)(2,1)S(1)}, bf16[2,4,64,640]{3,2,1,0:T(8,128)(2,1)S(1)}, u32[]{:S(2)}, u32[]{:S(2)}) collective-permute-start(bf16[2,4,64,640]{3,2,1,0:T(8,128)(2,1)S(1)} %get-tuple-element.80), channel_id=1, source_target_pairs={{0,4},{1,5},{2,6},{3,7},{4,0},{5,1},{6,2},{7,3},{8,12},{9,13},{10,... | collective-permute-start | bytes 1966088 | tf_op jit(solution)/shard_map/ppermute | solution.py:95
  323.5 11.8 %collective-permute-start.45 = (bf16[2,64,640]{2,1,0:T(8,128)(2,1)S(1)}, bf16[2,64,640]{2,1,0:T(8,128)(2,1)S(1)}, u32[]{:S(2)}, u32[]{:S(2)}) collective-permute-start(bf16[2,64,640]{2,1,0:T(8,128)(2,1)S(1)} %get-tuple-element.97), channel_id=1, source_target_pairs={{0,8},{1,9},{2,10},{3,11},{4,12},{5,13},{6,14},{7,15},{8,16},{9,17... | collective-permute-start | bytes 491528 | tf_op jit(solution)/shard_map/ppermute | solution.py:95
  (61 other events, 581.7 us)
where the time goes:
time: 346 us; the launch traced here: 345 us
  waiting for transfers between devices  152 us (44%)
  starting transfers between devices  68.8 us (20%)
  Pallas kernels  56.5 us (16%)
  local copies, waits for them, and re-layouts  33.4 us (10%)
  other arithmetic  32.5 us (9%)
    ppermute x64, waiting for transfers between devices, _permute(): return lax.ppermute(value, AXES, pairs)  152 us
    ppermute x64, starting transfers between devices, _permute(): return lax.ppermute(value, AXES, pairs)  68.8 us
    pallas_call x4, Pallas kernels, run_kernel(): pl.pallas_call(body, out_shape=[jax.ShapeDtypeStruct(shape, kind) for sha...  56.5 us
  transfers between devices with their start and end apart: 64, of which 21 were waited for; matrix products, arithmetic and copies ran while one was open for 16% of the time, Pallas kernels for 12%

commit v1 on v0

--- a/solution.py
+++ b/solution.py
@@ -113,7 +113,7 @@
             jnp.concatenate([other, own], axis=axis),
         )
 
-    def gather_z(self, block):
+    def gather_z(self, block, axis):
         parts = [block] + [self.over_z(block, k) for k in range(1, self.nz)]
         slots = []
         for slot in range(self.nz):
@@ -122,12 +122,13 @@
             for k in range(1, self.nz):
                 value = jnp.where(distance == k, parts[k], value)
             slots.append(value)
-        return jnp.stack(slots, axis=1)
-
-    def spread(self, line):
+        return jnp.stack(slots, axis=axis)
+
+    def spread(self, line, axis):
         by_x = self.over_x(line)
         by_y = self.over_y(line)
-        corners = self.over_y(by_x[0]), self.over_x(by_y[1])
+        item = (slice(None),) * (1 - axis)
+        corners = self.over_y(by_x[item + (0,)]), self.over_x(by_y[item + (1,)])
         return line, by_x, by_y, *corners
 
     def reduce(self, parts):
@@ -202,7 +203,7 @@
         def store(t, y, z, x, piece, which=which):
             w_ref[which, y, z, x, t * 64 : (t + 1) * 64, :] = piece
 
-        assemble(store, x, y, nz, line, by_x, by_y, corner_0, corner_1)
+        assemble(store, x, y, nz, 0, line, by_x, by_y, corner_0, corner_1)
     gains = [[], []]
     for z in range(nz):
         for p in range(2):
@@ -289,14 +290,15 @@
     return [two, two, one, one, two]
 
 
-def assemble(store, x, y, nz, line, by_x, by_y, corner_0, corner_1):
+def assemble(store, x, y, nz, axis, line, by_x, by_y, corner_0, corner_1):
     @pl.loop(0, nz)
     def _(z):
         for t in range(2):
             corner = (corner_0, corner_1)[t]
             for dy in range(2):
                 for dx in range(2):
-                    piece = corner[z] if dy and dx else (line, by_x, by_y)[dx + 2 * dy][t, z]
+                    at = (z, t) if axis == 0 else (t, z)
+                    piece = corner[z] if dy and dx else (line, by_x, by_y)[dx + 2 * dy][at]
                     store(t, y ^ dy, z, x ^ dx, piece)
 
 
@@ -306,7 +308,7 @@
         def store(t, y, z, x, piece, which=which):
             w_ref[which, y, z, x, t * 64 : (t + 1) * 64, :] = piece
 
-        assemble(store, x, y, nz, *parts)
+        assemble(store, x, y, nz, which, *parts)
 
 
 def feed_forward(dims, place_ref, second_ref, got_ref, cot_ref, *refs):
@@ -348,7 +350,7 @@
     def store(t, y, z, x, piece):
         d_ref[y, z, x, t * part : (t + 1) * part, :] = piece
 
-    assemble(store, x, y, nz, *refs[10:15])
+    assemble(store, x, y, nz, 1, *refs[10:15])
     assemble_gate_up(w_ref, x, y, nz, refs[:5], refs[5:10])
     tokens = second_ref.shape[0]
     pair = jnp.concatenate([second_ref[...], got_ref[...]], axis=0)
@@ -573,15 +575,15 @@
     up_pack = chip_pack(tall(pick(c, up_half)), got[2])
     down_pack = w_down.reshape(2, ff_rows // 2, w_down.shape[1])
 
-    attn_line = net.gather_z(attn_pack)
-    gate_line = net.gather_z(gate_pack)
-    up_line = net.gather_z(up_pack)
-    down_line = net.gather_z(down_pack)
-    attn_own = net.spread(attn_line)
+    attn_line = net.gather_z(attn_pack, 0)
+    gate_line = net.gather_z(gate_pack, 0)
+    up_line = net.gather_z(up_pack, 1)
+    down_line = net.gather_z(down_pack, 1)
+    attn_own = net.spread(attn_line, 0)
     attn_other = [net.core(piece) for piece in attn_own]
-    gate_parts = net.spread(gate_line)
-    up_parts = net.spread(up_line)
-    down_parts = net.spread(down_line)
+    gate_parts = net.spread(gate_line, 0)
+    up_parts = net.spread(up_line, 1)
+    down_parts = net.spread(down_line, 1)
 
     place = jnp.stack([c, x, y]).astype(jnp.int32)
     both_rows = 2 * local_rows

time: 346 us -> 345 us (level)
  local copies, waits for them, and re-layouts: 33.4 us -> 26.1 us
  waiting for transfers between devices: 152 us -> 157 us
    ppermute x7 -> x0, local copies, waits for them, and re-layouts: 6.37 us -> none  [_permute(): return lax.ppermute(value, AXES, pairs)]
    ppermute x64, waiting for transfers between devices: 152 us -> 157 us  [_permute(): return lax.ppermute(value, AXES, pairs)]
  transfers between devices with their start and end apart: 64 -> 64, of which waited for: 21 -> 22; matrix products, arithmetic and copies ran while one was open for 16% -> 14% of each run, Pallas kernels for 12% -> 12%
where the time goes in v1:
time: 345 us; the launch traced here: 343 us
  waiting for transfers between devices  157 us (46%)
  starting transfers between devices  70.1 us (20%)
  Pallas kernels  56.4 us (16%)
  other arithmetic  31.7 us (9%)
  local copies, waits for them, and re-layouts  26.1 us (8%)
    ppermute x64, waiting for transfers between devices, _permute(): return lax.ppermute(value, AXES, pairs)  157 us
    ppermute x64, starting transfers between devices, _permute(): return lax.ppermute(value, AXES, pairs)  70.1 us
    pallas_call x4, Pallas kernels, run_kernel(): pl.pallas_call(body, out_shape=[jax.ShapeDtypeStruct(shape, kind) for sha...  56.4 us
  transfers between devices with their start and end apart: 64, of which 22 were waited for; matrix products, arithmetic and copies ran while one was open for 14% of the time, Pallas kernels for 12%

profile of v1, /device:TPU:0, one launch (start us, length us, event | category | flops | bytes accessed | tf_op | source)
XLA Modules:
  0.0 343.0 jit_solution(3858803260347289502)
XLA Ops:
  0.7 5.1 %collective-permute-start.30 = (bf16[2,80,480]{2,1,0:T(8,128)(2,1)}, bf16[2,80,480]{2,1,0:T(8,128)(2,1)S(1)}, u32[]{:S(2)}, u32[]{:S(2)}) collective-permute-start(bf16[2,80,480]{2,1,0:T(8,128)(2,1)} %bitcast.252), channel_id=1, source_target_pairs={{0,24},{1,25},{2,26},{3,27},{4,28},{5,29},{6,30},{7,31},{8,0},{9,1... | collective-permute-start | bytes 460808 | tf_op jit(solution)/shard_map/ppermute | solution.py:95
  11.0 1.6 collective-permute-start
  13.9 2.1 fusion.pad_ref
  20.1 1.6 collective-permute-start.33
  21.7 2.7 collective-permute-start.2
  26.9 2.8 collective-permute-start.23
  31.2 5.0 %collective-permute-start.24 = (bf16[2,64,640]{2,1,0:T(8,128)(2,1)S(1)}, bf16[2,64,640]{2,1,0:T(8,128)(2,1)S(1)}, u32[]{:S(2)}, u32[]{:S(2)}) collective-permute-start(bf16[2,64,640]{2,1,0:T(8,128)(2,1)S(1)} %maximum_select_fusion.2), channel_id=1, source_target_pairs={{0,16},{1,17},{2,18},{3,19},{4,20},{5,21},{6,22},{7,23},{8,24},{9,... | collective-permute-start | bytes 491528 | tf_op jit(solution)/shard_map/ppermute | solution.py:95
  36.2 8.5 %collective-permute-done.3 = bf16[2,64,640]{2,1,0:T(8,128)(2,1)S(1)} collective-permute-done((bf16[2,64,640]{2,1,0:T(8,128)(2,1)S(1)}, bf16[2,64,640]{2,1,0:T(8,128)(2,1)S(1)}, u32[]{:S(2)}, u32[]{:S(2)}) %collective-permute-start.3) | collective-permute-done | bytes 163872 | tf_op jit(solution)/shard_map/ppermute | solution.py:95
  44.7 3.8 %collective-permute-start.16 = (bf16[2,64,640]{2,1,0:T(8,128)(2,1)S(1)}, bf16[2,64,640]{2,1,0:T(8,128)(2,1)S(1)}, u32[]{:S(2)}, u32[]{:S(2)}) collective-permute-start(bf16[2,64,640]{2,1,0:T(8,128)(2,1)S(1)} %maximum_select_fusion.1), channel_id=1, source_target_pairs={{0,24},{1,25},{2,26},{3,27},{4,28},{5,29},{6,30},{7,31},{8,0},{9,1... | collective-permute-start | bytes 491528 | tf_op jit(solution)/shard_map/ppermute | solution.py:95
  48.7 2.6 collective-permute-start.17
  51.4 5.6 %collective-permute-done.24 = bf16[2,64,640]{2,1,0:T(8,128)(2,1)S(1)} collective-permute-done((bf16[2,64,640]{2,1,0:T(8,128)(2,1)S(1)}, bf16[2,64,640]{2,1,0:T(8,128)(2,1)S(1)}, u32[]{:S(2)}, u32[]{:S(2)}) %collective-permute-start.24) | collective-permute-done | bytes 163872 | tf_op jit(solution)/shard_map/ppermute | solution.py:95
  58.8 1.6 collective-permute-start.26
  60.3 8.2 %collective-permute-done.17 = bf16[2,64,640]{2,1,0:T(8,128)(2,1)S(1)} collective-permute-done((bf16[2,64,640]{2,1,0:T(8,128)(2,1)S(1)}, bf16[2,64,640]{2,1,0:T(8,128)(2,1)S(1)}, u32[]{:S(2)}, u32[]{:S(2)}) %collective-permute-start.17) | collective-permute-done | bytes 163872 | tf_op jit(solution)/shard_map/ppermute | solution.py:95
  69.0 1.5 collective-permute-start.6
  72.2 3.4 collective-permute-done.5.refs_1_
  76.1 24.1 %collective-permute-done.6.refs_2_ = bf16[4,2,64,640]{3,2,1,0:T(8,128)(2,1)S(1)} collective-permute-done((bf16[4,2,64,640]{3,2,1,0:T(8,128)(2,1)S(1)}, bf16[4,2,64,640]{3,2,1,0:T(8,128)(2,1)S(1)}, u32[]{:S(2)}, u32[]{:S(2)}) %collective-permute-start.6) | collective-permute-done | bytes 655392 | tf_op jit(solution)/shard_map/ppermute | solution.py:95
  102.2 12.0 %collective-permute-done.20.refs_2_ = bf16[4,2,64,640]{3,2,1,0:T(8,128)(2,1)S(1)} collective-permute-done((bf16[4,2,64,640]{3,2,1,0:T(8,128)(2,1)S(1)}, bf16[4,2,64,640]{3,2,1,0:T(8,128)(2,1)S(1)}, u32[]{:S(2)}, u32[]{:S(2)}) %collective-permute-start.20) | collective-permute-done | bytes 655392 | tf_op jit(solution)/shard_map/ppermute | solution.py:95
  115.7 5.4 %collective-permute-done.7.refs_3_ = bf16[4,64,640]{2,1,0:T(8,128)(2,1)S(1)} collective-permute-done((bf16[4,64,640]{2,1,0:T(8,128)(2,1)S(1)}, bf16[4,64,640]{2,1,0:T(8,128)(2,1)S(1)}, u32[]{:S(2)}, u32[]{:S(2)}) %collective-permute-start.7) | collective-permute-done | bytes 327712 | tf_op jit(solution)/shard_map/ppermute | solution.py:95
  124.1 1.7 collective-permute-start.21
  128.1 12.6 %shard_map.186 = (bf16[2,2,4,2,128,640]{5,4,3,2,1,0:T(8,128)(2,1)}, bf16[2,1024,512]{2,1,0:T(8,128)(2,1)}, f32[8,1024]{1,0:T(8,128)}, bf16[256,1024]{1,0:T(8,128...) custom-call(s32[3]{0:T(128)} %pad_add_fusion.2.place_ref, ...), custom_call_target="tpu_custom_call" | custom-call | flops 2000000000 | bytes 8749068 | tf_op jit(solution)/shard_map/pallas_call | solution.py:500
  144.1 5.2 %collective-permute-done.21.refs_3_ = bf16[4,64,640]{2,1,0:T(8,128)(2,1)} collective-permute-done((bf16[4,64,640]{2,1,0:T(8,128)(2,1)}, bf16[4,64,640]{2,1,0:T(8,128)(2,1)}, u32[]{:S(2)}, u32[]{:S(2)}) %collective-permute-start.21) | collective-permute-done | bytes 327712 | tf_op jit(solution)/shard_map/ppermute | solution.py:95
  150.0 8.8 %shard_map.187 = (f32[2,256,640]{2,1,0:T(8,128)}, f32[2,256,640]{2,1,0:T(8,128)}, bf16[2,256,640]{2,1,0:T(8,128)(2,1)}, bf16[2,4,80,480]{3,2,1,0:T(8,128)(2,1)},...) custom-call(s32[3]{0:T(128)} %pad_add_fusion.2.place_ref, ...), custom_call_target="tpu_custom_call" | custom-call | flops 2000000000 | bytes 6258700 | tf_op jit(solution)/shard_map/pallas_call | solution.py:500
  159.7 16.2 %shard_map.188 = (f32[128,1024]{1,0:T(8,128)}, bf16[128,1024]{1,0:T(8,128)(2,1)}, f32[128,1024]{1,0:T(8,128)}, bf16[128,1024]{1,0:T(8,128)(2,1)}, bf16[2,4,2,64,...) custom-call(s32[3]{0:T(128)} %pad_add_fusion.2.place_ref, ...), custom_call_target="tpu_custom_call" | custom-call | flops 2000000000 | bytes 12484620 | tf_op jit(solution)/shard_map/pallas_call | solution.py:500
  178.3 1.6 collective-permute-start.49
  181.5 18.7 %shard_map.189 = (bf16[8,4,64,640]{3,2,1,0:T(8,128)(2,1)}, bf16[8,4,64,640]{3,2,1,0:T(8,128)(2,1)}, f32[128,1024]{1,0:T(8,128)}, f32[128,1024]{1,0:T(8,128)}, bf16[128,1024]{1,0:T(8,128)(2,1)}) custom-call(s32[3]{0:T(128)} %pad_add_fusion.2.place_ref, bf16[960,1024]{1,0:T(8,128)(2,1)} %fusion.pad_ref, bf16[128,960]{1,0:T(8,128)(2,1)} %bitcast.248, ...), custom_call_target="tpu_custom_call" | custom-call | flops 2000000000 | bytes 15024140 | tf_op jit(solution)/shard_map/pallas_call | solution.py:500
  203.2 24.9 %collective-permute-done.39 = bf16[128,1024]{1,0:T(8,128)(2,1)S(1)} collective-permute-done((bf16[128,1024]{1,0:T(8,128)(2,1)}, bf16[128,1024]{1,0:T(8,128)(2,1)S(1)}, u32[]{:S(2)}, u32[]{:S(2)}) %collective-permute-start.39) | collective-permute-done | bytes 262176 | tf_op jit(solution)/shard_map/ppermute | solution.py:95
  231.1 2.0 copy.88
  234.5 1.9 fusion.16
  236.9 1.8 fusion.15
  239.1 2.1 fusion.5
  242.7 2.1 fusion.4
  244.8 1.6 collective-permute-start.52
  247.3 2.4 collective-permute-done.60
  249.6 1.6 fusion.17
  251.6 9.3 %collective-permute-done.50 = bf16[4,2,64,640]{3,2,1,0:T(8,128)(2,1)} collective-permute-done((bf16[4,2,64,640]{3,2,1,0:T(8,128)(2,1)}, bf16[4,2,64,640]{3,2,1,0:T(8,128)(2,1)}, u32[]{:S(2)}, u32[]{:S(2)}) %collective-permute-start.50) | collective-permute-done | bytes 655392 | tf_op jit(solution)/shard_map/ppermute | solution.py:95
  260.8 2.1 collective-permute-done.52
  262.9 2.2 fusion.6
  265.7 4.0 %collective-permute-start.55 = (bf16[2,2,64,640]{3,2,1,0:T(8,128)(2,1)S(1)}, bf16[2,2,64,640]{3,2,1,0:T(8,128)(2,1)S(1)}, u32[]{:S(2)}, u32[]{:S(2)}) collective-permute-start(bf16[2,2,64,640]{3,2,1,0:T(8,128)(2,1)S(1)} %get-tuple-element.84), channel_id=1, source_target_pairs={{0,24},{1,25},{2,26},{3,27},{4,28},{5,29},{6,30},{7,31},{8,0},{9,1... | collective-permute-start | bytes 983048 | tf_op jit(solution)/shard_map/ppermute | solution.py:95
  271.5 6.5 %collective-permute-done.53 = bf16[2,2,64,640]{3,2,1,0:T(8,128)(2,1)S(1)} collective-permute-done((bf16[2,2,64,640]{3,2,1,0:T(8,128)(2,1)S(1)}, bf16[2,2,64,640]{3,2,1,0:T(8,128)(2,1)S(1)}, u32[]{:S(2)}, u32[]{:S(2)}) %collective-permute-start.53) | collective-permute-done | bytes 327712 | tf_op jit(solution)/shard_map/ppermute | solution.py:95
  278.0 12.5 %collective-permute-done.54 = bf16[2,2,64,640]{3,2,1,0:T(8,128)(2,1)S(1)} collective-permute-done((bf16[2,2,64,640]{3,2,1,0:T(8,128)(2,1)S(1)}, bf16[2,2,64,640]{3,2,1,0:T(8,128)(2,1)S(1)}, u32[]{:S(2)}, u32[]{:S(2)}) %collective-permute-start.54) | collective-permute-done | bytes 327712 | tf_op jit(solution)/shard_map/ppermute | solution.py:95
  293.9 1.8 collective-permute-start.43
  295.9 13.6 %collective-permute-done.41 = bf16[2,4,64,640]{3,2,1,0:T(8,128)(2,1)S(1)} collective-permute-done((bf16[2,4,64,640]{3,2,1,0:T(8,128)(2,1)S(1)}, bf16[2,4,64,640]{3,2,1,0:T(8,128)(2,1)S(1)}, u32[]{:S(2)}, u32[]{:S(2)}) %collective-permute-start.41) | collective-permute-done | bytes 655392 | tf_op jit(solution)/shard_map/ppermute | solution.py:95
  310.7 1.5 collective-permute-start.42
  312.3 1.6 collective-permute-start.44
  315.0 3.8 %collective-permute-done.42 = bf16[4,64,640]{2,1,0:T(8,128)(2,1)S(1)} collective-permute-done((bf16[4,64,640]{2,1,0:T(8,128)(2,1)}, bf16[4,64,640]{2,1,0:T(8,128)(2,1)S(1)}, u32[]{:S(2)}, u32[]{:S(2)}) %collective-permute-start.42) | collective-permute-done | bytes 327712 | tf_op jit(solution)/shard_map/ppermute | solution.py:95
  322.2 7.0 %collective-permute-start.45 = (bf16[2,64,640]{2,1,0:T(8,128)(2,1)S(1)}, bf16[2,64,640]{2,1,0:T(8,128)(2,1)S(1)}, u32[]{:S(2)}, u32[]{:S(2)}) collective-permute-start(bf16[2,64,640]{2,1,0:T(8,128)(2,1)S(1)} %get-tuple-element.97), channel_id=1, source_target_pairs={{0,8},{1,9},{2,10},{3,11},{4,12},{5,13},{6,14},{7,15},{8,16},{9,17... | collective-permute-start | bytes 491528 | tf_op jit(solution)/shard_map/ppermute | solution.py:95
  329.2 2.4 collective-permute-start.47
  333.6 5.1 %collective-permute-done.46 = bf16[2,64,640]{2,1,0:T(8,128)(2,1)S(1)} collective-permute-done((bf16[2,64,640]{2,1,0:T(8,128)(2,1)S(1)}, bf16[2,64,640]{2,1,0:T(8,128)(2,1)S(1)}, u32[]{:S(2)}, u32[]{:S(2)}) %collective-permute-start.46) | collective-permute-done | bytes 163872 | tf_op jit(solution)/shard_map/ppermute | solution.py:95
  (304 shorter events, 64.9 us)
Async XLA Ops:
  0.7 19.0 %collective-permute-start.30 = (bf16[2,80,480]{2,1,0:T(8,128)(2,1)}, bf16[2,80,480]{2,1,0:T(8,128)(2,1)S(1)}, u32[]{:S(2)}, u32[]{:S(2)}) collective-permute-start(bf16[2,80,480]{2,1,0:T(8,128)(2,1)} %bitcast.252), channel_id=1, source_target_pairs={{0,24},{1,25},{2,26},{3,27},{4,28},{5,29},{6,30},{7,31},{8,0},{9,1... | collective-permute-start | bytes 460808 | tf_op jit(solution)/shard_map/ppermute | solution.py:95
  5.8 14.1 %collective-permute-start.31 = (bf16[2,80,480]{2,1,0:T(8,128)(2,1)}, bf16[2,80,480]{2,1,0:T(8,128)(2,1)S(1)}, u32[]{:S(2)}, u32[]{:S(2)}) collective-permute-start(bf16[2,80,480]{2,1,0:T(8,128)(2,1)} %bitcast.253), channel_id=1, source_target_pairs={{0,16},{1,17},{2,18},{3,19},{4,20},{5,21},{6,22},{7,23},{8,24},{9,... | collective-permute-start | bytes 460808 | tf_op jit(solution)/shard_map/ppermute | solution.py:95
  5.8 14.1 %collective-permute-start.32 = (bf16[2,80,480]{2,1,0:T(8,128)(2,1)}, bf16[2,80,480]{2,1,0:T(8,128)(2,1)S(1)}, u32[]{:S(2)}, u32[]{:S(2)}) collective-permute-start(bf16[2,80,480]{2,1,0:T(8,128)(2,1)} %bitcast.254), channel_id=1, source_target_pairs={{0,8},{1,9},{2,10},{3,11},{4,12},{5,13},{6,14},{7,15},{8,16},{9,17... | collective-permute-start | bytes 460808 | tf_op jit(solution)/shard_map/ppermute | solution.py:95
  11.0 15.9 %collective-permute-start = (bf16[136,960]{1,0:T(8,128)(2,1)S(1)}, bf16[136,960]{1,0:T(8,128)(2,1)S(1)}, u32[]{:S(2)}, u32[]{:S(2)}) collective-permute-start(bf16[136,960]{1,0:T(8,128)(2,1)S(1)} %fusion.37), channel_id=1, source_target_pairs={{0,1},{1,0},{2,3},{3,2},{4,5},{5,4},{6,7},{7,6},{8,9},{9,8},{10,11... | collective-permute-start | bytes 783368 | tf_op jit(solution)/shard_map/ppermute | solution.py:95
  20.1 50.7 %collective-permute-start.33 = (bf16[2,4,80,480]{3,2,1,0:T(8,128)(2,1)S(1)}, bf16[2,4,80,480]{3,2,1,0:T(8,128)(2,1)S(1)}, u32[]{:S(2)}, u32[]{:S(2)}) collective-permute-start(bf16[2,4,80,480]{3,2,1,0:T(8,128)(2,1)S(1)} %pad_maximum_fusion.6.refs_10_), channel_id=1, source_target_pairs={{0,4},{1,5},{2,6},{3,7},{4,0},{5,1},{6,2},{7,3},{8,12},{9,13},{10,... | collective-permute-start | bytes 1843208 | tf_op jit(solution)/shard_map/ppermute | solution.py:95
  24.4 20.2 %collective-permute-start.3 = (bf16[2,64,640]{2,1,0:T(8,128)(2,1)S(1)}, bf16[2,64,640]{2,1,0:T(8,128)(2,1)S(1)}, u32[]{:S(2)}, u32[]{:S(2)}) collective-permute-start(bf16[2,64,640]{2,1,0:T(8,128)(2,1)S(1)} %maximum_select_fusion), channel_id=1, source_target_pairs={{0,16},{1,17},{2,18},{3,19},{4,20},{5,21},{6,22},{7,23},{8,24},{9,... | collective-permute-start | bytes 491528 | tf_op jit(solution)/shard_map/ppermute | solution.py:95
  25.6 19.0 %collective-permute-start.4 = (bf16[2,64,640]{2,1,0:T(8,128)(2,1)S(1)}, bf16[2,64,640]{2,1,0:T(8,128)(2,1)S(1)}, u32[]{:S(2)}, u32[]{:S(2)}) collective-permute-start(bf16[2,64,640]{2,1,0:T(8,128)(2,1)S(1)} %maximum_select_fusion), channel_id=1, source_target_pairs={{0,8},{1,9},{2,10},{3,11},{4,12},{5,13},{6,14},{7,15},{8,16},{9,17... | collective-permute-start | bytes 491528 | tf_op jit(solution)/shard_map/ppermute | solution.py:95
  26.9 21.8 %collective-permute-start.23 = (bf16[2,64,640]{2,1,0:T(8,128)(2,1)S(1)}, bf16[2,64,640]{2,1,0:T(8,128)(2,1)S(1)}, u32[]{:S(2)}, u32[]{:S(2)}) collective-permute-start(bf16[2,64,640]{2,1,0:T(8,128)(2,1)S(1)} %maximum_select_fusion.2), channel_id=1, source_target_pairs={{0,24},{1,25},{2,26},{3,27},{4,28},{5,29},{6,30},{7,31},{8,0},{9,1... | collective-permute-start | bytes 491528 | tf_op jit(solution)/shard_map/ppermute | solution.py:95
  31.2 25.8 %collective-permute-start.24 = (bf16[2,64,640]{2,1,0:T(8,128)(2,1)S(1)}, bf16[2,64,640]{2,1,0:T(8,128)(2,1)S(1)}, u32[]{:S(2)}, u32[]{:S(2)}) collective-permute-start(bf16[2,64,640]{2,1,0:T(8,128)(2,1)S(1)} %maximum_select_fusion.2), channel_id=1, source_target_pairs={{0,16},{1,17},{2,18},{3,19},{4,20},{5,21},{6,22},{7,23},{8,24},{9,... | collective-permute-start | bytes 491528 | tf_op jit(solution)/shard_map/ppermute | solution.py:95
  44.6 13.3 %collective-permute-start.25 = (bf16[2,64,640]{2,1,0:T(8,128)(2,1)S(1)}, bf16[2,64,640]{2,1,0:T(8,128)(2,1)S(1)}, u32[]{:S(2)}, u32[]{:S(2)}) collective-permute-start(bf16[2,64,640]{2,1,0:T(8,128)(2,1)S(1)} %maximum_select_fusion.2), channel_id=1, source_target_pairs={{0,8},{1,9},{2,10},{3,11},{4,12},{5,13},{6,14},{7,15},{8,16},{9,17... | collective-permute-start | bytes 491528 | tf_op jit(solution)/shard_map/ppermute | solution.py:95
  44.7 14.1 %collective-permute-start.16 = (bf16[2,64,640]{2,1,0:T(8,128)(2,1)S(1)}, bf16[2,64,640]{2,1,0:T(8,128)(2,1)S(1)}, u32[]{:S(2)}, u32[]{:S(2)}) collective-permute-start(bf16[2,64,640]{2,1,0:T(8,128)(2,1)S(1)} %maximum_select_fusion.1), channel_id=1, source_target_pairs={{0,24},{1,25},{2,26},{3,27},{4,28},{5,29},{6,30},{7,31},{8,0},{9,1... | collective-permute-start | bytes 491528 | tf_op jit(solution)/shard_map/ppermute | solution.py:95
  48.7 19.8 %collective-permute-start.17 = (bf16[2,64,640]{2,1,0:T(8,128)(2,1)S(1)}, bf16[2,64,640]{2,1,0:T(8,128)(2,1)S(1)}, u32[]{:S(2)}, u32[]{:S(2)}) collective-permute-start(bf16[2,64,640]{2,1,0:T(8,128)(2,1)S(1)} %maximum_select_fusion.1), channel_id=1, source_target_pairs={{0,16},{1,17},{2,18},{3,19},{4,20},{5,21},{6,22},{7,23},{8,24},{9,... | collective-permute-start | bytes 491528 | tf_op jit(solution)/shard_map/ppermute | solution.py:95
  57.0 12.0 %collective-permute-start.18 = (bf16[2,64,640]{2,1,0:T(8,128)(2,1)S(1)}, bf16[2,64,640]{2,1,0:T(8,128)(2,1)S(1)}, u32[]{:S(2)}, u32[]{:S(2)}) collective-permute-start(bf16[2,64,640]{2,1,0:T(8,128)(2,1)S(1)} %maximum_select_fusion.1), channel_id=1, source_target_pairs={{0,8},{1,9},{2,10},{3,11},{4,12},{5,13},{6,14},{7,15},{8,16},{9,17... | collective-permute-start | bytes 491528 | tf_op jit(solution)/shard_map/ppermute | solution.py:95
  58.0 17.6 %collective-permute-start.5 = (bf16[4,2,64,640]{3,2,1,0:T(8,128)(2,1)S(1)}, bf16[4,2,64,640]{3,2,1,0:T(8,128)(2,1)S(1)}, u32[]{:S(2)}, u32[]{:S(2)}) collective-permute-start(bf16[4,2,64,640]{3,2,1,0:T(8,128)(2,1)S(1)} %pad_maximum_fusion.3.refs_0_), channel_id=1, source_target_pairs={{0,4},{1,5},{2,6},{3,7},{4,0},{5,1},{6,2},{7,3},{8,12},{9,13},{10,... | collective-permute-start | bytes 1966088 | tf_op jit(solution)/shard_map/ppermute | solution.py:95
  58.8 41.5 %collective-permute-start.26 = (bf16[2,4,64,640]{3,2,1,0:T(8,128)(2,1)S(1)}, bf16[2,4,64,640]{3,2,1,0:T(8,128)(2,1)S(1)}, u32[]{:S(2)}, u32[]{:S(2)}) collective-permute-start(bf16[2,4,64,640]{3,2,1,0:T(8,128)(2,1)S(1)} %pad_maximum_fusion.5.refs_5_), channel_id=1, source_target_pairs={{0,4},{1,5},{2,6},{3,7},{4,0},{5,1},{6,2},{7,3},{8,12},{9,13},{10,... | collective-permute-start | bytes 1966088 | tf_op jit(solution)/shard_map/ppermute | solution.py:95
  68.5 32.3 %collective-permute-start.27 = (bf16[2,4,64,640]{3,2,1,0:T(8,128)(2,1)S(1)}, bf16[2,4,64,640]{3,2,1,0:T(8,128)(2,1)S(1)}, u32[]{:S(2)}, u32[]{:S(2)}) collective-permute-start(bf16[2,4,64,640]{3,2,1,0:T(8,128)(2,1)S(1)} %pad_maximum_fusion.5.refs_5_), channel_id=1, source_target_pairs={{0,1},{1,0},{2,3},{3,2},{4,5},{5,4},{6,7},{7,6},{8,9},{9,8},{10,11... | collective-permute-start | bytes 1966088 | tf_op jit(solution)/shard_map/ppermute | solution.py:95
  69.0 31.1 %collective-permute-start.6 = (bf16[4,2,64,640]{3,2,1,0:T(8,128)(2,1)S(1)}, bf16[4,2,64,640]{3,2,1,0:T(8,128)(2,1)S(1)}, u32[]{:S(2)}, u32[]{:S(2)}) collective-permute-start(bf16[4,2,64,640]{3,2,1,0:T(8,128)(2,1)S(1)} %pad_maximum_fusion.3.refs_0_), channel_id=1, source_target_pairs={{0,1},{1,0},{2,3},{3,2},{4,5},{5,4},{6,7},{7,6},{8,9},{9,8},{10,11... | collective-permute-start | bytes 1966088 | tf_op jit(solution)/shard_map/ppermute | solution.py:95
  70.8 31.3 %collective-permute-start.19 = (bf16[4,2,64,640]{3,2,1,0:T(8,128)(2,1)S(1)}, bf16[4,2,64,640]{3,2,1,0:T(8,128)(2,1)S(1)}, u32[]{:S(2)}, u32[]{:S(2)}) collective-permute-start(bf16[4,2,64,640]{3,2,1,0:T(8,128)(2,1)S(1)} %pad_maximum_fusion.4.refs_0_), channel_id=1, source_target_pairs={{0,4},{1,5},{2,6},{3,7},{4,0},{5,1},{6,2},{7,3},{8,12},{9,13},{10,... | collective-permute-start | bytes 1966088 | tf_op jit(solution)/shard_map/ppermute | solution.py:95
  75.6 38.6 %collective-permute-start.20 = (bf16[4,2,64,640]{3,2,1,0:T(8,128)(2,1)S(1)}, bf16[4,2,64,640]{3,2,1,0:T(8,128)(2,1)S(1)}, u32[]{:S(2)}, u32[]{:S(2)}) collective-permute-start(bf16[4,2,64,640]{3,2,1,0:T(8,128)(2,1)S(1)} %pad_maximum_fusion.4.refs_0_), channel_id=1, source_target_pairs={{0,1},{1,0},{2,3},{3,2},{4,5},{5,4},{6,7},{7,6},{8,9},{9,8},{10,11... | collective-permute-start | bytes 1966088 | tf_op jit(solution)/shard_map/ppermute | solution.py:95
  100.2 14.9 %collective-permute-start.9 = (bf16[4,2,64,640]{3,2,1,0:T(8,128)(2,1)S(1)}, bf16[4,2,64,640]{3,2,1,0:T(8,128)(2,1)S(1)}, u32[]{:S(2)}, u32[]{:S(2)}) collective-permute-start(bf16[4,2,64,640]{3,2,1,0:T(8,128)(2,1)S(1)} %pad_maximum_fusion.3.refs_0_), channel_id=1, source_target_pairs={{0,2},{1,3},{2,0},{3,1},{4,6},{5,7},{6,4},{7,5},{8,10},{9,11},{10,... | collective-permute-start | bytes 1966088 | tf_op jit(solution)/shard_map/ppermute | solution.py:95
  100.2 20.8 %collective-permute-start.7 = (bf16[4,64,640]{2,1,0:T(8,128)(2,1)S(1)}, bf16[4,64,640]{2,1,0:T(8,128)(2,1)S(1)}, u32[]{:S(2)}, u32[]{:S(2)}) collective-permute-start(bf16[4,64,640]{2,1,0:T(8,128)(2,1)S(1)} %slice_bitcast_fusion.11), channel_id=1, source_target_pairs={{0,1},{1,0},{2,3},{3,2},{4,5},{5,4},{6,7},{7,6},{8,9},{9,8},{10,11... | collective-permute-start | bytes 983048 | tf_op jit(solution)/shard_map/ppermute | solution.py:95
  100.8 20.3 %collective-permute-start.8 = (bf16[4,64,640]{2,1,0:T(8,128)(2,1)S(1)}, bf16[4,64,640]{2,1,0:T(8,128)(2,1)S(1)}, u32[]{:S(2)}, u32[]{:S(2)}) collective-permute-start(bf16[4,64,640]{2,1,0:T(8,128)(2,1)S(1)} %slice_bitcast_fusion.10), channel_id=1, source_target_pairs={{0,4},{1,5},{2,6},{3,7},{4,0},{5,1},{6,2},{7,3},{8,12},{9,13},{10,... | collective-permute-start | bytes 983048 | tf_op jit(solution)/shard_map/ppermute | solution.py:95
  102.1 22.0 %collective-permute-start.10 = (bf16[4,2,64,640]{3,2,1,0:T(8,128)(2,1)S(1)}, bf16[4,2,64,640]{3,2,1,0:T(8,128)(2,1)S(1)}, u32[]{:S(2)}, u32[]{:S(2)}) collective-permute-start(bf16[4,2,64,640]{3,2,1,0:T(8,128)(2,1)S(1)} %collective-permute-done.5.refs_1_), channel_id=1, source_target_pairs={{0,2},{1,3},{2,0},{3,1},{4,6},{5,7},{6,4},{7,5},{8,10},{9,11},{10,... | collective-permute-start | bytes 1966088 | tf_op jit(solution)/shard_map/ppermute | solution.py:95
  114.2 11.5 %collective-permute-start.11 = (bf16[4,2,64,640]{3,2,1,0:T(8,128)(2,1)S(1)}, bf16[4,2,64,640]{3,2,1,0:T(8,128)(2,1)S(1)}, u32[]{:S(2)}, u32[]{:S(2)}) collective-permute-start(bf16[4,2,64,640]{3,2,1,0:T(8,128)(2,1)S(1)} %collective-permute-done.6.refs_2_), channel_id=1, source_target_pairs={{0,2},{1,3},{2,0},{3,1},{4,6},{5,7},{6,4},{7,5},{8,10},{9,11},{10,... | collective-permute-start | bytes 1966088 | tf_op jit(solution)/shard_map/ppermute | solution.py:95
  115.1 25.7 %collective-permute-start.34 = (bf16[2,4,80,480]{3,2,1,0:T(8,128)(2,1)S(1)}, bf16[2,4,80,480]{3,2,1,0:T(8,128)(2,1)S(1)}, u32[]{:S(2)}, u32[]{:S(2)}) collective-permute-start(bf16[2,4,80,480]{3,2,1,0:T(8,128)(2,1)S(1)} %pad_maximum_fusion.6.refs_10_), channel_id=1, source_target_pairs={{0,1},{1,0},{2,3},{3,2},{4,5},{5,4},{6,7},{7,6},{8,9},{9,8},{10,11... | collective-permute-start | bytes 1843208 | tf_op jit(solution)/shard_map/ppermute | solution.py:95
  123.1 19.1 %collective-permute-start.28 = (bf16[4,64,640]{2,1,0:T(8,128)(2,1)}, bf16[4,64,640]{2,1,0:T(8,128)(2,1)}, u32[]{:S(2)}, u32[]{:S(2)}) collective-permute-start(bf16[4,64,640]{2,1,0:T(8,128)(2,1)} %slice_bitcast_fusion.7), channel_id=1, source_target_pairs={{0,1},{1,0},{2,3},{3,2},{4,5},{5,4},{6,7},{7,6},{8,9},{9,8},{10,11... | collective-permute-start | bytes 983048 | tf_op jit(solution)/shard_map/ppermute | solution.py:95
  123.5 19.1 %collective-permute-start.29 = (bf16[4,64,640]{2,1,0:T(8,128)(2,1)}, bf16[4,64,640]{2,1,0:T(8,128)(2,1)}, u32[]{:S(2)}, u32[]{:S(2)}) collective-permute-start(bf16[4,64,640]{2,1,0:T(8,128)(2,1)} %slice_bitcast_fusion.6), channel_id=1, source_target_pairs={{0,4},{1,5},{2,6},{3,7},{4,0},{5,1},{6,2},{7,3},{8,12},{9,13},{10,... | collective-permute-start | bytes 983048 | tf_op jit(solution)/shard_map/ppermute | solution.py:95
  124.1 25.2 %collective-permute-start.21 = (bf16[4,64,640]{2,1,0:T(8,128)(2,1)}, bf16[4,64,640]{2,1,0:T(8,128)(2,1)}, u32[]{:S(2)}, u32[]{:S(2)}) collective-permute-start(bf16[4,64,640]{2,1,0:T(8,128)(2,1)} %slice_bitcast_fusion.9), channel_id=1, source_target_pairs={{0,1},{1,0},{2,3},{3,2},{4,5},{5,4},{6,7},{7,6},{8,9},{9,8},{10,11... | collective-permute-start | bytes 983048 | tf_op jit(solution)/shard_map/ppermute | solution.py:95
  126.6 22.6 %collective-permute-start.22 = (bf16[4,64,640]{2,1,0:T(8,128)(2,1)}, bf16[4,64,640]{2,1,0:T(8,128)(2,1)}, u32[]{:S(2)}, u32[]{:S(2)}) collective-permute-start(bf16[4,64,640]{2,1,0:T(8,128)(2,1)} %slice_bitcast_fusion.8), channel_id=1, source_target_pairs={{0,4},{1,5},{2,6},{3,7},{4,0},{5,1},{6,2},{7,3},{8,12},{9,13},{10,... | collective-permute-start | bytes 983048 | tf_op jit(solution)/shard_map/ppermute | solution.py:95
  142.2 16.6 %collective-permute-start.35 = (bf16[4,80,480]{2,1,0:T(8,128)(2,1)}, bf16[4,80,480]{2,1,0:T(8,128)(2,1)S(1)}, u32[]{:S(2)}, u32[]{:S(2)}) collective-permute-start(bf16[4,80,480]{2,1,0:T(8,128)(2,1)} %slice_bitcast_fusion.5), channel_id=1, source_target_pairs={{0,1},{1,0},{2,3},{3,2},{4,5},{5,4},{6,7},{7,6},{8,9},{9,8},{10,11... | collective-permute-start | bytes 921608 | tf_op jit(solution)/shard_map/ppermute | solution.py:95
  142.6 16.2 %collective-permute-start.36 = (bf16[4,80,480]{2,1,0:T(8,128)(2,1)S(1)}, bf16[4,80,480]{2,1,0:T(8,128)(2,1)S(1)}, u32[]{:S(2)}, u32[]{:S(2)}) collective-permute-start(bf16[4,80,480]{2,1,0:T(8,128)(2,1)S(1)} %slice_bitcast_fusion.4), channel_id=1, source_target_pairs={{0,4},{1,5},{2,6},{3,7},{4,0},{5,1},{6,2},{7,3},{8,12},{9,13},{10,... | collective-permute-start | bytes 921608 | tf_op jit(solution)/shard_map/ppermute | solution.py:95
  176.0 24.2 %collective-permute-start.37 = (bf16[128,1024]{1,0:T(8,128)(2,1)}, bf16[128,1024]{1,0:T(8,128)(2,1)S(1)}, u32[]{:S(2)}, u32[]{:S(2)}) collective-permute-start(bf16[128,1024]{1,0:T(8,128)(2,1)} %get-tuple-element.49), channel_id=1, source_target_pairs={{0,2},{1,3},{2,0},{3,1},{4,6},{5,7},{6,4},{7,5},{8,10},{9,11},{10,... | collective-permute-start | bytes 786440 | tf_op jit(solution)/shard_map/ppermute | solution.py:95
  177.3 57.1 %collective-permute-start.57 = (bf16[2,4,80,480]{3,2,1,0:T(8,128)(2,1)}, bf16[2,4,80,480]{3,2,1,0:T(8,128)(2,1)}, u32[]{:S(2)}, u32[]{:S(2)}) collective-permute-start(bf16[2,4,80,480]{3,2,1,0:T(8,128)(2,1)} %get-tuple-element.72), channel_id=1, source_target_pairs={{0,1},{1,0},{2,3},{3,2},{4,5},{5,4},{6,7},{7,6},{8,9},{9,8},{10,11... | collective-permute-start | bytes 1843208 | tf_op jit(solution)/shard_map/ppermute | solution.py:95
  177.8 59.1 %collective-permute-start.59 = (bf16[2,4,80,480]{3,2,1,0:T(8,128)(2,1)}, bf16[2,4,80,480]{3,2,1,0:T(8,128)(2,1)}, u32[]{:S(2)}, u32[]{:S(2)}) collective-permute-start(bf16[2,4,80,480]{3,2,1,0:T(8,128)(2,1)} %get-tuple-element.74), channel_id=1, source_target_pairs={{0,4},{1,5},{2,6},{3,7},{4,0},{5,1},{6,2},{7,3},{8,12},{9,13},{10,... | collective-permute-start | bytes 1843208 | tf_op jit(solution)/shard_map/ppermute | solution.py:95
  178.3 60.8 %collective-permute-start.49 = (bf16[2,4,2,64,640]{4,3,2,1,0:T(8,128)(2,1)}, bf16[2,4,2,64,640]{4,3,2,1,0:T(8,128)(2,1)}, u32[]{:S(2)}, u32[]{:S(2)}) collective-permute-start(bf16[2,4,2,64,640]{4,3,2,1,0:T(8,128)(2,1)} %get-tuple-element.67), channel_id=1, source_target_pairs={{0,1},{1,0},{2,3},{3,2},{4,5},{5,4},{6,7},{7,6},{8,9},{9,8},{10,11... | collective-permute-start | bytes 3932168 | tf_op jit(solution)/shard_map/ppermute | solution.py:95
  180.0 62.7 %collective-permute-start.51 = (bf16[2,4,2,64,640]{4,3,2,1,0:T(8,128)(2,1)}, bf16[2,4,2,64,640]{4,3,2,1,0:T(8,128)(2,1)}, u32[]{:S(2)}, u32[]{:S(2)}) collective-permute-start(bf16[2,4,2,64,640]{4,3,2,1,0:T(8,128)(2,1)} %get-tuple-element.69), channel_id=1, source_target_pairs={{0,4},{1,5},{2,6},{3,7},{4,0},{5,1},{6,2},{7,3},{8,12},{9,13},{10,... | collective-permute-start | bytes 3932168 | tf_op jit(solution)/shard_map/ppermute | solution.py:95
  200.2 27.9 %collective-permute-start.39 = (bf16[128,1024]{1,0:T(8,128)(2,1)}, bf16[128,1024]{1,0:T(8,128)(2,1)S(1)}, u32[]{:S(2)}, u32[]{:S(2)}) collective-permute-start(bf16[128,1024]{1,0:T(8,128)(2,1)} %get-tuple-element.63), channel_id=1, source_target_pairs={{0,1},{1,0},{2,3},{3,2},{4,5},{5,4},{6,7},{7,6},{8,9},{9,8},{10,11... | collective-permute-start | bytes 786440 | tf_op jit(solution)/shard_map/ppermute | solution.py:95
  228.1 62.7 %collective-permute-start.40 = (bf16[8,4,64,640]{3,2,1,0:T(8,128)(2,1)}, bf16[8,4,64,640]{3,2,1,0:T(8,128)(2,1)S(1)}, u32[]{:S(2)}, u32[]{:S(2)}) collective-permute-start(bf16[8,4,64,640]{3,2,1,0:T(8,128)(2,1)} %get-tuple-element.65), channel_id=1, source_target_pairs={{0,2},{1,3},{2,0},{3,1},{4,6},{5,7},{6,4},{7,5},{8,10},{9,11},{10,... | collective-permute-start | bytes 7864328 | tf_op jit(solution)/shard_map/ppermute | solution.py:95
  241.2 19.6 %collective-permute-start.50 = (bf16[4,2,64,640]{3,2,1,0:T(8,128)(2,1)}, bf16[4,2,64,640]{3,2,1,0:T(8,128)(2,1)}, u32[]{:S(2)}, u32[]{:S(2)}) collective-permute-start(bf16[4,2,64,640]{3,2,1,0:T(8,128)(2,1)} %fusion.5), channel_id=1, source_target_pairs={{0,4},{1,5},{2,6},{3,7},{4,0},{5,1},{6,2},{7,3},{8,12},{9,13},{10,... | collective-permute-start | bytes 1966088 | tf_op jit(solution)/shard_map/ppermute | solution.py:95
  244.8 18.1 %collective-permute-start.52 = (bf16[4,2,64,640]{3,2,1,0:T(8,128)(2,1)}, bf16[4,2,64,640]{3,2,1,0:T(8,128)(2,1)}, u32[]{:S(2)}, u32[]{:S(2)}) collective-permute-start(bf16[4,2,64,640]{3,2,1,0:T(8,128)(2,1)} %fusion.4), channel_id=1, source_target_pairs={{0,1},{1,0},{2,3},{3,2},{4,5},{5,4},{6,7},{7,6},{8,9},{9,8},{10,11... | collective-permute-start | bytes 1966088 | tf_op jit(solution)/shard_map/ppermute | solution.py:95
  251.4 14.2 %collective-permute-start.61 = (bf16[2,80,480]{2,1,0:T(8,128)(2,1)S(1)}, bf16[2,80,480]{2,1,0:T(8,128)(2,1)S(1)}, u32[]{:S(2)}, u32[]{:S(2)}) collective-permute-start(bf16[2,80,480]{2,1,0:T(8,128)(2,1)S(1)} %get-tuple-element.88), channel_id=1, source_target_pairs={{0,8},{1,9},{2,10},{3,11},{4,12},{5,13},{6,14},{7,15},{8,16},{9,17... | collective-permute-start | bytes 460808 | tf_op jit(solution)/shard_map/ppermute | solution.py:95
  251.5 14.2 %collective-permute-start.62 = (bf16[2,80,480]{2,1,0:T(8,128)(2,1)S(1)}, bf16[2,80,480]{2,1,0:T(8,128)(2,1)S(1)}, u32[]{:S(2)}, u32[]{:S(2)}) collective-permute-start(bf16[2,80,480]{2,1,0:T(8,128)(2,1)S(1)} %get-tuple-element.90), channel_id=1, source_target_pairs={{0,16},{1,17},{2,18},{3,19},{4,20},{5,21},{6,22},{7,23},{8,24},{9,... | collective-permute-start | bytes 460808 | tf_op jit(solution)/shard_map/ppermute | solution.py:95
  265.5 12.5 %collective-permute-start.53 = (bf16[2,2,64,640]{3,2,1,0:T(8,128)(2,1)S(1)}, bf16[2,2,64,640]{3,2,1,0:T(8,128)(2,1)S(1)}, u32[]{:S(2)}, u32[]{:S(2)}) collective-permute-start(bf16[2,2,64,640]{3,2,1,0:T(8,128)(2,1)S(1)} %get-tuple-element.83), channel_id=1, source_target_pairs={{0,8},{1,9},{2,10},{3,11},{4,12},{5,13},{6,14},{7,15},{8,16},{9,17... | collective-permute-start | bytes 983048 | tf_op jit(solution)/shard_map/ppermute | solution.py:95
  265.6 24.9 %collective-permute-start.54 = (bf16[2,2,64,640]{3,2,1,0:T(8,128)(2,1)S(1)}, bf16[2,2,64,640]{3,2,1,0:T(8,128)(2,1)S(1)}, u32[]{:S(2)}, u32[]{:S(2)}) collective-permute-start(bf16[2,2,64,640]{3,2,1,0:T(8,128)(2,1)S(1)} %get-tuple-element.85), channel_id=1, source_target_pairs={{0,16},{1,17},{2,18},{3,19},{4,20},{5,21},{6,22},{7,23},{8,24},{9,... | collective-permute-start | bytes 983048 | tf_op jit(solution)/shard_map/ppermute | solution.py:95
  265.7 24.9 %collective-permute-start.55 = (bf16[2,2,64,640]{3,2,1,0:T(8,128)(2,1)S(1)}, bf16[2,2,64,640]{3,2,1,0:T(8,128)(2,1)S(1)}, u32[]{:S(2)}, u32[]{:S(2)}) collective-permute-start(bf16[2,2,64,640]{3,2,1,0:T(8,128)(2,1)S(1)} %get-tuple-element.84), channel_id=1, source_target_pairs={{0,24},{1,25},{2,26},{3,27},{4,28},{5,29},{6,30},{7,31},{8,0},{9,1... | collective-permute-start | bytes 983048 | tf_op jit(solution)/shard_map/ppermute | solution.py:95
  293.7 15.7 %collective-permute-start.41 = (bf16[2,4,64,640]{3,2,1,0:T(8,128)(2,1)S(1)}, bf16[2,4,64,640]{3,2,1,0:T(8,128)(2,1)S(1)}, u32[]{:S(2)}, u32[]{:S(2)}) collective-permute-start(bf16[2,4,64,640]{3,2,1,0:T(8,128)(2,1)S(1)} %get-tuple-element.81), channel_id=1, source_target_pairs={{0,1},{1,0},{2,3},{3,2},{4,5},{5,4},{6,7},{7,6},{8,9},{9,8},{10,11... | collective-permute-start | bytes 1966088 | tf_op jit(solution)/shard_map/ppermute | solution.py:95
  293.9 15.6 %collective-permute-start.43 = (bf16[2,4,64,640]{3,2,1,0:T(8,128)(2,1)S(1)}, bf16[2,4,64,640]{3,2,1,0:T(8,128)(2,1)S(1)}, u32[]{:S(2)}, u32[]{:S(2)}) collective-permute-start(bf16[2,4,64,640]{3,2,1,0:T(8,128)(2,1)S(1)} %get-tuple-element.80), channel_id=1, source_target_pairs={{0,4},{1,5},{2,6},{3,7},{4,0},{5,1},{6,2},{7,3},{8,12},{9,13},{10,... | collective-permute-start | bytes 1966088 | tf_op jit(solution)/shard_map/ppermute | solution.py:95
  322.2 11.4 %collective-permute-start.45 = (bf16[2,64,640]{2,1,0:T(8,128)(2,1)S(1)}, bf16[2,64,640]{2,1,0:T(8,128)(2,1)S(1)}, u32[]{:S(2)}, u32[]{:S(2)}) collective-permute-start(bf16[2,64,640]{2,1,0:T(8,128)(2,1)S(1)} %get-tuple-element.97), channel_id=1, source_target_pairs={{0,8},{1,9},{2,10},{3,11},{4,12},{5,13},{6,14},{7,15},{8,16},{9,17... | collective-permute-start | bytes 491528 | tf_op jit(solution)/shard_map/ppermute | solution.py:95
  (67 other events, 772.5 us)
